TPU v7x, 128 devices: a whole 4x4x4 slice. The times are simulated.
128 devices in a mesh: rep: 4 (over y_lo, core), fsdp: 32 (over x, z, y_hi).
Axes of the slice: x: 4, y: 4 (y_hi: 2, y_lo: 2; y = y_hi * 2 + y_lo), z: 4, core: 2. Of those that a mesh axis runs over, the one named last changes fastest.
Arguments:
- acts: bfloat16 [65536, 8192], P(('rep', 'fsdp')), may hold values from -24 to 24
- tok_grads: bfloat16 [65536, 1024], P(('rep', 'fsdp')), may hold values from -64 to 64
- log_ratio: float32 [65536], P(('rep', 'fsdp')), may hold values from -3 to 3
- loss_mask: int32 [65536], P(('rep', 'fsdp')), may hold values 0 or 1
- pairs: int32 [4, 32], P('rep'), may hold values from 0 to 31, each once within a row
- inner_w: float32 [4, 8192, 1024], P('rep', 'fsdp'), may hold values from -6 to 6
- adam_m: float32 [4, 8192, 1024], P('rep', 'fsdp'), may hold values from -3 to 3
- adam_v: float32 [4, 8192, 1024], P('rep', 'fsdp'), may hold values from 0.05 to 1
- anchor: float32 [8192, 1024], P('fsdp'), may hold values from -6 to 6
- outer_mom: float32 [8192, 1024], P('fsdp'), may hold values from -1.75 to 1.75
Outputs:
- input_grad: bfloat16 [65536, 8192], P(('rep', 'fsdp'))
- new_anchor: float32 [8192, 1024], P('fsdp')
- new_mom: float32 [8192, 1024], P('fsdp')
- new_m: float32 [4, 8192, 1024], P('rep', 'fsdp')
Inputs may be any that keep to these rules, and one draw needn't show every extreme that they name: Each row of pairs is a permutation of 0 to 31; chosen sequence c of a group pairs with rejected sequence 32 + pairs[r, c].
All inputs are finite; a program needn't handle non-finite values. No bound on the sum of `loss_mask` on one device may be relied on, other than what follows from the above.
Results may differ from a plain program's by a relative error of at most 0.0057.
Values may be sent and summed in bfloat16 or wider, within the bound.
No kernel may reach another device: no remote copies, remote signals or barrier semaphores. Data moves between devices by JAX's collectives and lax.ppermute only.
A program may use at most 128 MiB of HBM per device.

v0:
```python
import functools

import jax
import jax.numpy as jnp
from jax import lax
from jax.experimental import pallas as pl
from jax.experimental.pallas import tpu as pltpu
from jax.sharding import PartitionSpec as P


D = 8192
KVW = 1024
SEQLEN = 256
SEQ_DEV = 2
ROWS = SEQ_DEV * SEQLEN
HALF = 32
SHARD = 256

dpo_beta = 0.1
decay_one = 0.9
decay_two = 0.95
inner_rate = 0.05
weight_decay = 0.1
epsilon = 1e-08
momentum = 0.9
outer_rate = 0.7
SCALE = D ** (-0.5)


GRANT = 24 << 20


def send(value, target):
    pairs = []
    for f in range(32):
        x, z, y = target(f // 8, (f // 2) % 4, f % 2)
        pairs.append((f, (x % 4) * 8 + (z % 4) * 2 + y % 2))
    return lax.ppermute(value, "fsdp", pairs)


def shift(value, dx=0, dz=0, dy=0):
    return send(value, lambda x, z, y: (x + dx, z + dz, y + dy))


def send_tilted(value, step, far):
    pairs = []
    for i in range(128):
        rep, f = i // 32, i % 32
        x, z, y = f // 8, (f // 2) % 4, f % 2
        if (rep + y + far) % 2:
            z = (z + step) % 4
        else:
            x = (x + step) % 4
        pairs.append((i, rep * 32 + x * 8 + z * 2 + y))
    return lax.ppermute(value, ("rep", "fsdp"), pairs)


def shift_near(value, step):
    return send_tilted(value, step, 0)


def shift_far(value, step):
    return send_tilted(value, step, 1)


def swap_rep(value, bit):
    return lax.ppermute(value, "rep", [(r, r ^ bit) for r in range(4)])


def owner(x, z, y):
    return (x % 4) * 8 + (z % 4) * 2 + y


def sums_kernel(f_ref, ratio_ref, mask_ref, row_ref):
    kept = ratio_ref[...] * mask_ref[...].astype(jnp.float32)
    lane = lax.broadcasted_iota(jnp.int32, (1, 128), 1)
    row = jnp.zeros((1, 128), jnp.float32)
    rows = kept.shape[0] // SEQ_DEV
    for i in range(SEQ_DEV):
        part = jnp.sum(kept[i * rows : (i + 1) * rows], axis=0, keepdims=True)
        part = jnp.sum(part, axis=1, keepdims=True)
        row = jnp.where(lane == f_ref[0] * SEQ_DEV + i, part, row)
    row_ref[...] = row


def seq_sums(f, ratio, mask):
    vmem = pl.BlockSpec(memory_space=pltpu.VMEM)
    return pl.pallas_call(
        sums_kernel,
        out_shape=jax.ShapeDtypeStruct((1, 128), jnp.float32),
        in_specs=[pl.BlockSpec(memory_space=pltpu.SMEM), vmem, vmem],
        out_specs=vmem,
        compiler_params=pltpu.CompilerParams(vmem_limit_bytes=1 << 20),
        cost_estimate=pl.CostEstimate(flops=2048, transcendentals=0, bytes_accessed=4096),
        name="seq_sums",
    )(f, ratio, mask)


def cot_kernel(f_ref, v0_ref, v1_ref, v2_ref, v3_ref, pairs_ref, mrow_ref, mcol_ref, tg_ref, tgt_ref, cot_ref, cott_ref):
    f = f_ref[0]
    v = v0_ref[...] + v1_ref[...] + v2_ref[...] + v3_ref[...]
    row = lax.broadcasted_iota(jnp.int32, (HALF, 128), 0)
    lane = lax.broadcasted_iota(jnp.int32, (HALF, 128), 1)
    onehot = pairs_ref[...] == row
    rejected_col = jnp.sum(jnp.where(lane == row + HALF, v, 0.0), axis=1, keepdims=True)
    rejected = jnp.sum(jnp.where(onehot, rejected_col, 0.0), axis=0, keepdims=True)
    pull = jax.nn.sigmoid(-(dpo_beta * (v - rejected)))
    push = jnp.sum(jnp.where(onehot, pull, 0.0), axis=1, keepdims=True)
    lane_row = lax.broadcasted_iota(jnp.int32, (1, 128), 1)
    row_col = lax.broadcasted_iota(jnp.int32, (HALF, 1), 0)
    weights = []
    for i in range(SEQ_DEV):
        seq = f * SEQ_DEV + i
        chosen = jnp.sum(jnp.where(lane_row == seq, pull, 0.0), axis=1, keepdims=True)
        other = jnp.sum(jnp.where(row_col == seq - HALF, push, 0.0), axis=0, keepdims=True)
        weights.append(jnp.where(seq < HALF, -dpo_beta * chosen, dpo_beta * other))
    tok = lax.broadcasted_iota(jnp.int32, (1, ROWS), 1)
    wrow = jnp.where(tok < SEQLEN, weights[0], weights[1]) * mrow_ref[...]
    cott_ref[...] = (wrow * tgt_ref[...].astype(jnp.float32)).astype(jnp.bfloat16)
    for i in range(SEQ_DEV):
        part = slice(i * SEQLEN, (i + 1) * SEQLEN)
        wcol = weights[i] * mcol_ref[part, :]
        cot_ref[part, :] = (wcol * tg_ref[part, :].astype(jnp.float32)).astype(jnp.bfloat16)


def make_cot(f, rows, pairs_pad, mrow, mcol, tg, tgt):
    vmem = pl.BlockSpec(memory_space=pltpu.VMEM)
    return pl.pallas_call(
        cot_kernel,
        out_shape=(
            jax.ShapeDtypeStruct((ROWS, KVW), jnp.bfloat16),
            jax.ShapeDtypeStruct((KVW, ROWS), jnp.bfloat16),
        ),
        in_specs=[pl.BlockSpec(memory_space=pltpu.SMEM)] + [vmem] * 9,
        out_specs=(vmem, vmem),
        compiler_params=pltpu.CompilerParams(vmem_limit_bytes=GRANT),
        cost_estimate=pl.CostEstimate(flops=4_000_000, transcendentals=128, bytes_accessed=4 << 20),
        name="make_cot",
    )(f, *rows, pairs_pad, mrow, mcol, tg, tgt)


def term(cott_ref, acts_refs):
    acts = jnp.concatenate([a[...] for a in acts_refs], axis=1)
    return jnp.dot(cott_ref[...], acts, preferred_element_type=jnp.float32) * SCALE


def split_kernel(tab, cott_ref, a0, a1, *outs):
    t = term(cott_ref, (a0, a1)).astype(jnp.bfloat16)
    for colour in range(2):
        @pl.when(pl.program_id(0) // 2 == colour)
        def _(colour=colour):
            outs[2 * colour][...] = t[: KVW // 2]
            outs[2 * colour + 1][...] = t[KVW // 2 :]


def rest_kernel(tab, cott_ref, a0, a1, *outs):
    t = term(cott_ref, (a0, a1)).astype(jnp.bfloat16)
    for i, out in enumerate(outs):
        @pl.when(pl.program_id(0) // 2 == i)
        def _(out=out):
            out[...] = t


def products(kernel, first, count, rows, split, tab, cott, acts):
    spec = [
        pl.BlockSpec((rows, 2 * SHARD), lambda s, b, i=i: (0, jnp.clip(s - 2 * i, 0, 1)))
        for i in range(count)
        for _ in range(split)
    ]
    return pl.pallas_call(
        kernel,
        out_shape=(jax.ShapeDtypeStruct((rows, 4 * SHARD), jnp.bfloat16),) * (count * split),
        grid_spec=pltpu.PrefetchScalarGridSpec(
            num_scalar_prefetch=1,
            grid=(2 * count,),
            in_specs=[
                pl.BlockSpec((KVW, ROWS), lambda s, b: (0, 0)),
                pl.BlockSpec((ROWS, SHARD), lambda s, b: (0, b[first + 2 * s])),
                pl.BlockSpec((ROWS, SHARD), lambda s, b: (0, b[first + 2 * s + 1])),
            ],
            out_specs=tuple(spec),
        ),
        compiler_params=pltpu.CompilerParams(
            dimension_semantics=("arbitrary",), vmem_limit_bytes=GRANT
        ),
        cost_estimate=pl.CostEstimate(
            flops=2 * KVW * ROWS * 4 * SHARD * count, transcendentals=0, bytes_accessed=count * (3 << 20)
        ),
    )(tab, cott, acts, acts)


def input_grad_kernel(edges, tab, cot_ref, *rest):
    out_ref = rest[-1]
    for i, (low, high) in enumerate(edges):
        @pl.when((pl.program_id(0) >= low) & (pl.program_id(0) < high))
        def _(w_ref=rest[i]):
            t = lax.dot_general(
                cot_ref[...], w_ref[...], (((1,), (1,)), ((), ())), preferred_element_type=jnp.float32
            )
            out_ref[...] = (t * SCALE).astype(jnp.bfloat16)


def input_grad_part(first, tab, cot, pieces, previous):
    edges, n = [], 0
    for piece in pieces:
        edges.append((n, n + piece.shape[0] // SHARD))
        n = edges[-1][1]
    aliased = [] if previous is None else [previous]
    return pl.pallas_call(
        functools.partial(input_grad_kernel, tuple(edges)),
        out_shape=jax.ShapeDtypeStruct((ROWS, D), jnp.bfloat16),
        grid_spec=pltpu.PrefetchScalarGridSpec(
            num_scalar_prefetch=1,
            grid=(n,),
            in_specs=[pl.BlockSpec((ROWS, KVW), lambda s, b: (0, 0))]
            + [
                pl.BlockSpec((SHARD, KVW), lambda s, b, e=e: (jnp.clip(s - e[0], 0, e[1] - e[0] - 1), 0))
                for e in edges
            ]
            + [pl.BlockSpec(memory_space=pl.ANY)] * len(aliased),
            out_specs=pl.BlockSpec((ROWS, SHARD), lambda s, b: (0, b[first + s])),
        ),
        input_output_aliases={2 + len(pieces): 0} if aliased else {},
        compiler_params=pltpu.CompilerParams(
            dimension_semantics=("arbitrary",), vmem_limit_bytes=GRANT
        ),
        cost_estimate=pl.CostEstimate(
            flops=2 * KVW * ROWS * n * SHARD, transcendentals=0, bytes_accessed=(1 << 20) + n * (3 << 18)
        ),
        name="input_grad",
    )(tab, cot, *pieces, *aliased)


def choose_kernel(my_ref, *refs):
    first, second = [
        sum(r[...].astype(jnp.float32) for r in refs[4 * c : 4 * c + 4]).astype(jnp.bfloat16) for c in (0, 1)
    ]
    keep_ref, give_ref = refs[8:]
    upper = my_ref[0] == 1
    keep_ref[...] = jnp.where(upper, second, first)
    give_ref[...] = jnp.where(upper, first, second)


def choose(my, parts):
    block = pl.BlockSpec((256, SHARD), lambda i: (i, 0))
    return pl.pallas_call(
        choose_kernel,
        grid=(KVW // 256,),
        out_shape=(jax.ShapeDtypeStruct((KVW, SHARD), jnp.bfloat16),) * 2,
        in_specs=[pl.BlockSpec(memory_space=pltpu.SMEM)] + [block] * 8,
        out_specs=(block, block),
        compiler_params=pltpu.CompilerParams(vmem_limit_bytes=GRANT),
        cost_estimate=pl.CostEstimate(flops=2 << 20, transcendentals=0, bytes_accessed=5 << 20),
        name="choose",
    )(my, *parts)


def adam_kernel(keep_ref, recv_ref, m_ref, v_ref, w_ref, anchor_ref, m_out, delta_out):
    grad = (keep_ref[...].astype(jnp.float32) + recv_ref[...].astype(jnp.float32)).T
    w = w_ref[0]
    m_next = decay_one * m_ref[0] + (1.0 - decay_one) * grad
    v_next = decay_two * v_ref[0] + (1.0 - decay_two) * grad * grad
    inner_next = w - inner_rate * (m_next / (jnp.sqrt(v_next) + epsilon) + weight_decay * w)
    m_out[0] = m_next
    delta_out[...] = anchor_ref[...] - inner_next


def adam(keep, recv, m, v, w, anchor):
    col = 128
    gt = pl.BlockSpec((col, SHARD), lambda j: (j, 0))
    cube = pl.BlockSpec((1, SHARD, col), lambda j: (0, 0, j))
    flat = pl.BlockSpec((SHARD, col), lambda j: (0, j))
    return pl.pallas_call(
        adam_kernel,
        grid=(KVW // col,),
        out_shape=(
            jax.ShapeDtypeStruct((1, SHARD, KVW), jnp.float32),
            jax.ShapeDtypeStruct((SHARD, KVW), jnp.float32),
        ),
        in_specs=[gt, gt, cube, cube, cube, flat],
        out_specs=(cube, flat),
        compiler_params=pltpu.CompilerParams(vmem_limit_bytes=GRANT),
        cost_estimate=pl.CostEstimate(flops=20 << 18, transcendentals=2 << 18, bytes_accessed=7 << 20),
        name="adam",
    )(keep, recv, m, v, w, anchor)


def local(acts, tok_grads, log_ratio, loss_mask, pairs, inner_w, adam_m, adam_v, anchor, outer_mom):
    f = lax.axis_index("fsdp")
    mx, mz, my = f // 8, (f // 2) % 4, f % 2
    core = lax.axis_index("rep") % 2
    bf16, f32 = jnp.bfloat16, jnp.float32

    in_hbm = lambda value: pltpu.with_memory_space_constraint(value, pltpu.HBM)
    acts = in_hbm(acts)

    def far0(k):
        return [owner(mx + k, mz + j, 0) for j in range(4)]

    def far1(k):
        return [owner(mx + j, mz + k, 1) for j in range(4)]

    tilt = (core + my) % 2

    def gathered(who, k, js):
        axis, plane = (tilt, my) if who == "own" else (1 - tilt, 1 - my)
        return [
            jnp.where(axis == 0, owner(mx + j, mz + k, plane), owner(mx + k, mz + j, plane)) for j in js
        ]

    entries = far0(2) + far1(2) + far0(1) + far0(3) + far1(1) + far1(3) + far0(0) + far1(0)
    starts = []
    every, low, high = range(4), (0, 1), (2, 3)
    for group in (
        [("own", 0, every), ("oth", 0, every), ("own", 1, high), ("own", 3, low)],
        [("own", 1, low), ("own", 3, high), ("oth", 1, high), ("oth", 3, low)],
        [("oth", 1, low), ("oth", 3, high), ("own", 2, every)],
        [("oth", 2, every)],
    ):
        starts.append(len(entries))
        for entry in group:
            entries = entries + gathered(*entry)
    tab = jnp.stack(entries).astype(jnp.int32)

    mask_f = loss_mask.astype(f32)
    where_f = f.reshape(1).astype(jnp.int32)
    row = seq_sums(where_f, log_ratio.reshape(ROWS // 128, 128), loss_mask.reshape(ROWS // 128, 128))
    row = row + shift(row, dy=1)
    row = row + shift(row, dx=1) + shift(row, dx=-1) + shift(row, dx=2)
    rows = (row, shift(row, dz=1), shift(row, dz=-1), shift(row, dz=2))

    w_half = inner_w[0].astype(bf16)
    one, two, three = shift_near(w_half, -1), shift_near(w_half, 2), shift_near(w_half, 1)
    row_low = jnp.concatenate([w_half, one], axis=0)
    row_high = jnp.concatenate([two, three], axis=0)
    other_low, other_high = shift(row_low, dy=1), shift(row_high, dy=1)
    next_high, prev_low = shift_far(row_high, -1), shift_far(row_low, 1)
    next_low, prev_high = shift_far(row_low, -1), shift_far(row_high, 1)
    rest = (shift(next_high, dy=1), shift(prev_low, dy=1))
    relay = (shift_far(next_low, -1), shift_far(prev_high, 1))
    cross = (shift_near(other_low, -1), shift_near(other_high, 1))
    last = (shift_near(cross[0], -1), shift_near(cross[1], 1))

    pairs_pad = jnp.pad(pairs, ((0, 0), (0, 128 - HALF)), constant_values=-1)
    cot, cott = make_cot(
        where_f, rows, pairs_pad, mask_f.reshape(1, ROWS), mask_f.reshape(ROWS, 1),
        tok_grads, tok_grads.T,
    )

    def big(colour, value, step):
        return shift(value, dx=step) if colour == 0 else shift(value, dz=step)

    def small(colour, value, step):
        return shift(value, dz=step) if colour == 0 else shift(value, dx=step)

    h = KVW // 2
    ups = products(split_kernel, 0, 2, h, 2, tab, cott, acts)
    terms = products(rest_kernel, 8, 6, KVW, 1, tab, cott, acts)
    sums = []
    relayed = []
    for c in (0, 1):
        relayed.append((big(c, ups[2 * c], 1), big(c, ups[2 * c + 1], -1)))
    got = []
    for c in (0, 1):
        plus = terms[2 * c].at[:h].add(relayed[c][0])
        minus = terms[2 * c + 1].at[h:].add(relayed[c][1])
        got.append((big(c, plus, 1), big(c, minus, -1)))
    for c in (0, 1):
        parts = []
        for k in range(4):
            cols = slice(k * SHARD, (k + 1) * SHARD)
            part = terms[4 + c][:, cols].astype(f32)
            part = part + got[c][0][:, cols].astype(f32) + got[c][1][:, cols].astype(f32)
            parts.append(part.astype(bf16))
        moved = [small(c, parts[k], step) for k, step in ((1, 1), (2, 2), (3, -1))]
        sums += [parts[0]] + moved
    keep, give = choose(my.reshape(1).astype(jnp.int32), sums)
    recv = in_hbm(shift(in_hbm(give), dy=1))
    new_m, delta = adam(keep, recv, in_hbm(adam_m), in_hbm(adam_v), in_hbm(inner_w), in_hbm(anchor))

    hs = SHARD // 2
    part = jnp.where(core == 0, delta[:hs], delta[hs:])
    other = jnp.where(core == 0, delta[hs:], delta[:hs])
    part = part + swap_rep(other, 1)
    part = part + swap_rep(part, 2)
    other = swap_rep(part, 1)
    total = jnp.concatenate([jnp.where(core == 0, part, other), jnp.where(core == 0, other, part)], axis=0)
    delta_avg = total / 4
    new_mom = momentum * outer_mom + delta_avg
    new_anchor = anchor - outer_rate * (delta_avg + momentum * new_mom)

    groups = (
        (row_low, row_high, other_low, other_high, next_high, prev_low),
        (next_low, prev_high) + rest,
        cross + relay,
        last,
    )
    out = None
    for i, group in enumerate(groups):
        out = input_grad_part(starts[i], tab, cot, group, out)
    return (out, new_anchor, new_mom, new_m)


def solution(mesh):
    return jax.shard_map(
        local,
        mesh=mesh,
        in_specs=(
            P(("rep", "fsdp"), None),
            P(("rep", "fsdp"), None),
            P(("rep", "fsdp")),
            P(("rep", "fsdp")),
            P("rep", None),
            P("rep", "fsdp", None),
            P("rep", "fsdp", None),
            P("rep", "fsdp", None),
            P("fsdp", None),
            P("fsdp", None),
        ),
        out_specs=(
            P(("rep", "fsdp"), None),
            P("fsdp", None),
            P("fsdp", None),
            P("rep", "fsdp", None),
        ),
        check_vma=False,
    )
```

profile of v0, /device:TPU:1, one launch (start us, length us, event | category | flops | bytes accessed | tf_op | source)
XLA Modules:
  0.0 282.1 jit_solution(3934083949627863930)
XLA Ops:
  0.7 0.8 copy-done.5
  1.4 0.7 copy-done.6
  2.2 3.7 %collective-permute-start = (f32[1,128]{1,0:T(1,128)S(1)}, f32[1,128]{1,0:T(1,128)S(1)}, u32[]{:S(2)}, u32[]{:S(2)}) collective-permute-start(f32[1,128]{1,0:T(1,128)S(1)} %seq_sums.1), channel_id=1, source_target_pairs={{0,1},{1,0},{2,3},{3,2},{4,5},{5,4},{6,7},{7,6},{8,9},{9,8},{10,11... | collective-permute-start | bytes 1544 | tf_op jit(solution)/shard_map/ppermute | solution.py:38
  5.9 1.0 collective-permute-done
  6.9 1.3 collective-permute-start.1
  8.2 1.4 collective-permute-start.2
  9.6 1.6 collective-permute-start.3
  11.2 0.7 convert_element_type.105
  12.0 1.5 copy.18
  13.6 1.7 collective-permute-start.4
  15.3 2.2 collective-permute-start.5
  17.5 1.2 collective-permute-start.6
  18.9 2.5 collective-permute-done.6.v3_ref
  21.4 0.7 make_cot.1
  22.1 5.7 %shard_map.130 = (bf16[512,1024]{1,0:T(8,128)(2,1)S(1)}, bf16[512,1024]{1,0:T(8,128)(2,1)S(1)}, bf16[512,1024]{1,0:T(8,128)(2,1)S(1)}, bf16[512,1024]{1,0:T(8,128)(2,1)S(1)}) custom-call(s32[64]{0:T(128)S(1)} %stack.259.tab, bf16[1024,512]{1,0:T(8,128)(2,1)S(1)} %get-tuple-element.69.cott_ref, bf16[512,8192]{1,0:T(8,128)(2,1)} %a1.3, bf16[512,8192]{1,0:T(8,128)(2,1)} %a1.3), custom_call_target="tpu_custom_call" | custom-call | flops 2147483648 | bytes 6291456 | tf_op jit(solution)/shard_map/pallas_call | solution.py:170
  28.3 2.4 collective-permute-start.26
  30.6 2.7 collective-permute-start.33
  33.3 14.6 %shard_map.129 = (bf16[1024,1024]{1,0:T(8,128)(2,1)S(1)}, bf16[1024,1024]{1,0:T(8,128)(2,1)S(1)}, bf16[1024,1024]{1,0:T(8,128)(2,1)S(1)}, bf16[1024,1024]{1,0:T(...) custom-call(s32[64]{0:T(128)S(1)} %stack.259.tab, ...), custom_call_target="tpu_custom_call" | custom-call | flops 6442450944 | bytes 18874368 | tf_op jit(solution)/shard_map/pallas_call | solution.py:170
  47.9 1.1 collective-permute-done.24
  49.0 0.5 add_dynamic-update-slice_fusion.3
  49.6 0.5 add_dynamic-update-slice_fusion.2
  50.2 2.7 collective-permute-start.27
  52.9 0.5 add_dynamic-update-slice_fusion.1
  53.5 0.5 add_dynamic-update-slice_fusion
  54.1 2.9 %collective-permute-start.34 = (bf16[1024,1024]{1,0:T(8,128)(2,1)S(1)}, bf16[1024,1024]{1,0:T(8,128)(2,1)S(1)}, u32[]{:S(2)}, u32[]{:S(2)}) collective-permute-start(bf16[1024,1024]{1,0:T(8,128)(2,1)S(1)} %add_dynamic-update-slice_fusion), channel_id=1, source_target_pairs={{0,6},{1,7},{2,0},{3,1},{4,2},{5,3},{6,4},{7,5},{8,14},{9,15},{10,... | collective-permute-start | bytes 6291464 | tf_op jit(solution)/shard_map/ppermute | solution.py:38
  57.2 35.9 %collective-permute-done.25 = bf16[1024,1024]{1,0:T(8,128)(2,1)S(1)} collective-permute-done((bf16[1024,1024]{1,0:T(8,128)(2,1)S(1)}, bf16[1024,1024]{1,0:T(8,128)(2,1)S(1)}, u32[]{:S(2)}, u32[]{:S(2)}) %collective-permute-start.25) | collective-permute-done | bytes 2097184 | tf_op jit(solution)/shard_map/ppermute | solution.py:38
  93.1 2.7 collective-permute-start.7
  95.8 0.7 add_convert_fusion.4
  96.5 8.2 %collective-permute-done.11 = bf16[256,1024]{1,0:T(8,128)(2,1)S(1)} collective-permute-done((bf16[256,1024]{1,0:T(8,128)(2,1)S(1)}, bf16[256,1024]{1,0:T(8,128)(2,1)S(1)}, u32[]{:S(2)}, u32[]{:S(2)}) %collective-permute-start.11) | collective-permute-done | bytes 524320 | tf_op jit(solution)/shard_map/ppermute | solution.py:55
  104.8 1.6 collective-permute-start.28
  106.4 5.8 %collective-permute-done.12 = bf16[256,1024]{1,0:T(8,128)(2,1)S(1)} collective-permute-done((bf16[256,1024]{1,0:T(8,128)(2,1)S(1)}, bf16[256,1024]{1,0:T(8,128)(2,1)S(1)}, u32[]{:S(2)}, u32[]{:S(2)}) %collective-permute-start.12) | collective-permute-done | bytes 524320 | tf_op jit(solution)/shard_map/ppermute | solution.py:55
  112.3 0.6 collective-permute-start.29
  113.0 1.5 collective-permute-start.13
  114.5 0.7 collective-permute-start.30
  115.2 0.7 add_convert_fusion
  116.0 7.5 %collective-permute-done.28.refs_1_ = bf16[1024,256]{1,0:T(8,128)(2,1)S(1)} collective-permute-done((bf16[1024,256]{1,0:T(8,128)(2,1)S(1)}, bf16[1024,256]{1,0:T(8,128)(2,1)S(1)}, u32[]{:S(2)}, u32[]{:S(2)}) %collective-permute-start.28) | collective-permute-done | bytes 524320 | tf_op jit(solution)/shard_map/ppermute | solution.py:38
  123.5 1.2 collective-permute-start.36
  124.7 10.6 %collective-permute-done.29.refs_2_ = bf16[1024,256]{1,0:T(8,128)(2,1)S(1)} collective-permute-done((bf16[1024,256]{1,0:T(8,128)(2,1)S(1)}, bf16[1024,256]{1,0:T(8,128)(2,1)S(1)}, u32[]{:S(2)}, u32[]{:S(2)}) %collective-permute-start.29) | collective-permute-done | bytes 524320 | tf_op jit(solution)/shard_map/ppermute | solution.py:38
  136.2 1.0 collective-permute-start.22
  137.2 5.8 %collective-permute-start.8 = (bf16[512,1024]{1,0:T(8,128)(2,1)S(1)}, bf16[512,1024]{1,0:T(8,128)(2,1)}, u32[]{:S(2)}, u32[]{:S(2)}) collective-permute-start(bf16[512,1024]{1,0:T(8,128)(2,1)S(1)} %pad_maximum_fusion.rest_0_), channel_id=1, source_target_pairs={{0,1},{1,0},{2,3},{3,2},{4,5},{5,4},{6,7},{7,6},{8,9},{9,8},{10,11... | collective-permute-start | bytes 3145736 | tf_op jit(solution)/shard_map/ppermute | solution.py:38
  143.1 7.7 %collective-permute-done.37.refs_7_ = bf16[1024,256]{1,0:T(8,128)(2,1)S(1)} collective-permute-done((bf16[1024,256]{1,0:T(8,128)(2,1)S(1)}, bf16[1024,256]{1,0:T(8,128)(2,1)S(1)}, u32[]{:S(2)}, u32[]{:S(2)}) %collective-permute-start.37) | collective-permute-done | bytes 524320 | tf_op jit(solution)/shard_map/ppermute | solution.py:38
  150.8 0.6 collective-permute-start.18
  151.4 0.6 choose.1
  152.0 0.8 copy-done.3
  152.8 1.0 copy-done.1
  153.8 14.2 %collective-permute-done.38.recv_ref = bf16[1024,256]{1,0:T(8,128)(2,1)S(1)} collective-permute-done((bf16[1024,256]{1,0:T(8,128)(2,1)S(1)}, bf16[1024,256]{1,0:T(8,128)(2,1)S(1)}, u32[]{:S(2)}, u32[]{:S(2)}) %collective-permute-start.38) | collective-permute-done | bytes 524320 | tf_op jit(solution)/shard_map/ppermute | solution.py:38
  168.0 0.8 copy-done.10
  168.8 3.3 %collective-permute-start.16 = (bf16[512,1024]{1,0:T(8,128)(2,1)S(1)}, bf16[512,1024]{1,0:T(8,128)(2,1)}, u32[]{:S(2)}, u32[]{:S(2)}) collective-permute-start(bf16[512,1024]{1,0:T(8,128)(2,1)S(1)} %pad_maximum_fusion.rest_0_), channel_id=1, source_target_pairs={{0,6},{1,25},{2,0},{3,27},{4,2},{5,29},{6,4},{7,31},{8,14},{9,1},{... | collective-permute-start | bytes 3145736 | tf_op jit(solution)/shard_map/ppermute | solution.py:55
  172.1 1.0 copy-done.4
  173.1 6.6 %adam.1 = (f32[1,256,1024]{2,1,0:T(8,128)}, f32[256,1024]{1,0:T(8,128)S(1)}) custom-call(bf16[1024,256]{1,0:T(8,128)(2,1)S(1)} %copy-done.4, bf16[1024,256]{1,0:T(8,128)(2,1)} %copy-done.10, f32[1,256,1024]{2,1,0:T(8,128)} %m_ref.1, f32[1,256,1024]{2,1,0:T(8,128)} %v_ref.1, f32[1,256,1024]{2,1,0:T(8,128)} %w_ref.1, f32[256,1024]{1,0:T(8,128)} %anchor_ref.1), custom_call_target="tpu_custom_call" | custom-call | flops 5242880 | bytes 7340032 | tf_op jit(solution)/shard_map/adam/pallas_call | solution.py:273
  179.8 10.1 %collective-permute-start.39 = (f32[128,1024]{1,0:T(8,128)S(1)}, f32[128,1024]{1,0:T(8,128)S(1)}, u32[]{:S(2)}, u32[]{:S(2)}) collective-permute-start(f32[128,1024]{1,0:T(8,128)S(1)} %slice_select_fusion), channel_id=1, source_target_pairs={{0,32},{32,0},{64,96},{96,64},{1,33},{33,1},{65,97},{97,65},{2,34}... | collective-permute-start | bytes 1572872 | tf_op jit(solution)/shard_map/ppermute | solution.py:67
  190.4 2.3 collective-permute-start.9
  192.7 2.9 %collective-permute-start.23 = (bf16[512,1024]{1,0:T(8,128)(2,1)}, bf16[512,1024]{1,0:T(8,128)(2,1)S(1)}, u32[]{:S(2)}, u32[]{:S(2)}) collective-permute-start(bf16[512,1024]{1,0:T(8,128)(2,1)} %collective-permute-done.22.rest_5_), channel_id=1, source_target_pairs={{0,1},{1,0},{2,3},{3,2},{4,5},{5,4},{6,7},{7,6},{8,9},{9,8},{10,11... | collective-permute-start | bytes 3145736 | tf_op jit(solution)/shard_map/ppermute | solution.py:38
  195.7 0.9 collective-permute-start.40
  196.6 19.6 %collective-permute-done.21.rest_2_ = bf16[512,1024]{1,0:T(8,128)(2,1)S(1)} collective-permute-done((bf16[512,1024]{1,0:T(8,128)(2,1)}, bf16[512,1024]{1,0:T(8,128)(2,1)S(1)}, u32[]{:S(2)}, u32[]{:S(2)}) %collective-permute-start.21) | collective-permute-done | bytes 1048608 | tf_op jit(solution)/shard_map/ppermute | solution.py:38
  216.3 2.7 collective-permute-start.17
  219.3 28.6 %collective-permute-done.40 = f32[128,1024]{1,0:T(8,128)S(1)} collective-permute-done((f32[128,1024]{1,0:T(8,128)S(1)}, f32[128,1024]{1,0:T(8,128)S(1)}, u32[]{:S(2)}, u32[]{:S(2)}) %collective-permute-start.40) | collective-permute-done | bytes 524320 | tf_op jit(solution)/shard_map/ppermute | solution.py:67
  248.0 2.6 collective-permute-start.10
  251.0 11.0 %input_grad.4.rest_4_ = bf16[512,8192]{1,0:T(8,128)(2,1)} custom-call(s32[64]{0:T(128)S(1)} %stack.259.tab, bf16[512,1024]{1,0:T(8,128)(2,1)S(1)} %get-tuple-element.68.cot_ref, bf16[512,1024]{1,0:T(8,128)(2,1)S(1)} %pad_maximum_fusion.rest_0_, bf16[512,1024]{1,0:T(8,128)(2,1)S(1)} %constant_dynamic-update-slice_fusion.rest_1_, ...), custom_call_target="tpu_custom_call" | custom-call | flops 3221225472 | bytes 10485760 | tf_op jit(solution)/shard_map/input_grad/pallas_call | solution.py:209
  262.1 7.5 %input_grad.5.rest_4_ = bf16[512,8192]{1,0:T(8,128)(2,1)} custom-call(s32[64]{0:T(128)S(1)} %stack.259.tab, bf16[512,1024]{1,0:T(8,128)(2,1)S(1)} %get-tuple-element.68.cot_ref, bf16[512,1024]{1,0:T(8,128)(2,1)} %collective-permute-done.16.rest_0_, bf16[512,1024]{1,0:T(8,128)(2,1)} %collective-permute-done.18.rest_1_, ...), custom_call_target="tpu_custom_call", output_to_operand_aliasing={{}: (6, {})} | custom-call | flops 2147483648 | bytes 7340032 | tf_op jit(solution)/shard_map/input_grad/pallas_call | solution.py:209
  269.6 5.8 %input_grad.6.rest_2_ = bf16[512,8192]{1,0:T(8,128)(2,1)} custom-call(s32[64]{0:T(128)S(1)} %stack.259.tab, bf16[512,1024]{1,0:T(8,128)(2,1)S(1)} %get-tuple-element.68.cot_ref, bf16[512,1024]{1,0:T(8,128)(2,1)S(1)} %collective-permute-done.9.rest_0_, bf16[512,1024]{1,0:T(8,128)(2,1)S(1)} %collective-permute-done.14.rest_1_, ...), custom_call_target="tpu_custom_call", output_to_operand_aliasing={{}: (6, {})} | custom-call | flops 2147483648 | bytes 7340032 | tf_op jit(solution)/shard_map/input_grad/pallas_call | solution.py:209
  275.5 3.4 %input_grad.7 = bf16[512,8192]{1,0:T(8,128)(2,1)} custom-call(s32[64]{0:T(128)S(1)} %stack.259.tab, bf16[512,1024]{1,0:T(8,128)(2,1)S(1)} %get-tuple-element.68.cot_ref, bf16[512,1024]{1,0:T(8,128)(2,1)S(1)} %collective-permute-done.10.rest_0_, bf16[512,1024]{1,0:T(8,128)(2,1)S(1)} %collective-permute-done.15.rest_1_, ...), custom_call_target="tpu_custom_call", output_to_operand_aliasing={{}: (4, {})} | custom-call | flops 1073741824 | bytes 4194304 | tf_op jit(solution)/shard_map/input_grad/pallas_call | solution.py:209
  279.0 1.1 copy-done.7
  280.4 1.7 multiply_subtract_fusion
  (76 shorter events, 4.2 us)
Async XLA Ops:
  0.6 20.8 %copy-start = (bf16[512,1024]{1,0:T(8,128)(2,1)S(1)}, bf16[512,1024]{1,0:T(8,128)(2,1)}, u32[]{:S(2)}) copy-start(bf16[512,1024]{1,0:T(8,128)(2,1)} %tg_ref.1) | copy-start | bytes 3145732
  0.6 0.8 copy-start.5
  1.4 0.7 copy-start.6
  2.1 11.4 %copy-start.11 = (s32[1,32]{1,0:T(1,128)S(1)}, s32[1,32]{1,0:T(1,128)}, u32[]{:S(2)}) copy-start(s32[1,32]{1,0:T(1,128)} %param.22) | copy-start | bytes 388
  2.2 4.7 %collective-permute-start = (f32[1,128]{1,0:T(1,128)S(1)}, f32[1,128]{1,0:T(1,128)S(1)}, u32[]{:S(2)}, u32[]{:S(2)}) collective-permute-start(f32[1,128]{1,0:T(1,128)S(1)} %seq_sums.1), channel_id=1, source_target_pairs={{0,1},{1,0},{2,3},{3,2},{4,5},{5,4},{6,7},{7,6},{8,9},{9,8},{10,11... | collective-permute-start | bytes 1544 | tf_op jit(solution)/shard_map/ppermute | solution.py:38
  6.9 6.6 %collective-permute-start.1 = (f32[1,128]{1,0:T(1,128)S(1)}, f32[1,128]{1,0:T(1,128)S(1)}, u32[]{:S(2)}, u32[]{:S(2)}) collective-permute-start(f32[1,128]{1,0:T(1,128)S(1)} %add.871), channel_id=1, source_target_pairs={{0,8},{1,9},{2,10},{3,11},{4,12},{5,13},{6,14},{7,15},{8,16},{9,17... | collective-permute-start | bytes 1544 | tf_op jit(solution)/shard_map/ppermute | solution.py:38
  8.2 5.4 %collective-permute-start.2 = (f32[1,128]{1,0:T(1,128)S(1)}, f32[1,128]{1,0:T(1,128)S(1)}, u32[]{:S(2)}, u32[]{:S(2)}) collective-permute-start(f32[1,128]{1,0:T(1,128)S(1)} %add.871), channel_id=1, source_target_pairs={{0,24},{1,25},{2,26},{3,27},{4,28},{5,29},{6,30},{7,31},{8,0},{9,1... | collective-permute-start | bytes 1544 | tf_op jit(solution)/shard_map/ppermute | solution.py:38
  9.6 4.0 %collective-permute-start.3 = (f32[1,128]{1,0:T(1,128)S(1)}, f32[1,128]{1,0:T(1,128)S(1)}, u32[]{:S(2)}, u32[]{:S(2)}) collective-permute-start(f32[1,128]{1,0:T(1,128)S(1)} %add.871), channel_id=1, source_target_pairs={{0,16},{1,17},{2,18},{3,19},{4,20},{5,21},{6,22},{7,23},{8,24},{9,... | collective-permute-start | bytes 1544 | tf_op jit(solution)/shard_map/ppermute | solution.py:38
  13.6 5.3 %collective-permute-start.4 = (f32[1,128]{1,0:T(1,128)S(1)}, f32[1,128]{1,0:T(1,128)S(1)}, u32[]{:S(2)}, u32[]{:S(2)}) collective-permute-start(f32[1,128]{1,0:T(1,128)S(1)} %add_add_fusion.v0_ref), channel_id=1, source_target_pairs={{0,2},{1,3},{2,4},{3,5},{4,6},{5,7},{6,0},{7,1},{8,10},{9,11},{10,... | collective-permute-start | bytes 1544 | tf_op jit(solution)/shard_map/ppermute | solution.py:38
  15.3 3.6 %collective-permute-start.5 = (f32[1,128]{1,0:T(1,128)S(1)}, f32[1,128]{1,0:T(1,128)S(1)}, u32[]{:S(2)}, u32[]{:S(2)}) collective-permute-start(f32[1,128]{1,0:T(1,128)S(1)} %add_add_fusion.v0_ref), channel_id=1, source_target_pairs={{0,6},{1,7},{2,0},{3,1},{4,2},{5,3},{6,4},{7,5},{8,14},{9,15},{10,... | collective-permute-start | bytes 1544 | tf_op jit(solution)/shard_map/ppermute | solution.py:38
  17.5 3.9 %collective-permute-start.6 = (f32[1,128]{1,0:T(1,128)S(1)}, f32[1,128]{1,0:T(1,128)S(1)}, u32[]{:S(2)}, u32[]{:S(2)}) collective-permute-start(f32[1,128]{1,0:T(1,128)S(1)} %add_add_fusion.v0_ref), channel_id=1, source_target_pairs={{0,4},{1,5},{2,6},{3,7},{4,0},{5,1},{6,2},{7,3},{8,12},{9,13},{10,... | collective-permute-start | bytes 1544 | tf_op jit(solution)/shard_map/ppermute | solution.py:38
  27.9 21.1 %collective-permute-start.24 = (bf16[512,1024]{1,0:T(8,128)(2,1)S(1)}, bf16[512,1024]{1,0:T(8,128)(2,1)S(1)}, u32[]{:S(2)}, u32[]{:S(2)}) collective-permute-start(bf16[512,1024]{1,0:T(8,128)(2,1)S(1)} %get-tuple-element.72), channel_id=1, source_target_pairs={{0,8},{1,9},{2,10},{3,11},{4,12},{5,13},{6,14},{7,15},{8,16},{9,17... | collective-permute-start | bytes 3145736 | tf_op jit(solution)/shard_map/ppermute | solution.py:38
  28.3 21.4 %collective-permute-start.26 = (bf16[512,1024]{1,0:T(8,128)(2,1)S(1)}, bf16[512,1024]{1,0:T(8,128)(2,1)S(1)}, u32[]{:S(2)}, u32[]{:S(2)}) collective-permute-start(bf16[512,1024]{1,0:T(8,128)(2,1)S(1)} %get-tuple-element.74), channel_id=1, source_target_pairs={{0,24},{1,25},{2,26},{3,27},{4,28},{5,29},{6,30},{7,31},{8,0},{9,1... | collective-permute-start | bytes 3145736 | tf_op jit(solution)/shard_map/ppermute | solution.py:38
  30.6 22.3 %collective-permute-start.31 = (bf16[512,1024]{1,0:T(8,128)(2,1)S(1)}, bf16[512,1024]{1,0:T(8,128)(2,1)S(1)}, u32[]{:S(2)}, u32[]{:S(2)}) collective-permute-start(bf16[512,1024]{1,0:T(8,128)(2,1)S(1)} %get-tuple-element.77), channel_id=1, source_target_pairs={{0,2},{1,3},{2,4},{3,5},{4,6},{5,7},{6,0},{7,1},{8,10},{9,11},{10,... | collective-permute-start | bytes 3145736 | tf_op jit(solution)/shard_map/ppermute | solution.py:38
  30.6 22.9 %collective-permute-start.33 = (bf16[512,1024]{1,0:T(8,128)(2,1)S(1)}, bf16[512,1024]{1,0:T(8,128)(2,1)S(1)}, u32[]{:S(2)}, u32[]{:S(2)}) collective-permute-start(bf16[512,1024]{1,0:T(8,128)(2,1)S(1)} %get-tuple-element.79), channel_id=1, source_target_pairs={{0,6},{1,7},{2,0},{3,1},{4,2},{5,3},{6,4},{7,5},{8,14},{9,15},{10,... | collective-permute-start | bytes 3145736 | tf_op jit(solution)/shard_map/ppermute | solution.py:38
  49.5 43.6 %collective-permute-start.25 = (bf16[1024,1024]{1,0:T(8,128)(2,1)S(1)}, bf16[1024,1024]{1,0:T(8,128)(2,1)S(1)}, u32[]{:S(2)}, u32[]{:S(2)}) collective-permute-start(bf16[1024,1024]{1,0:T(8,128)(2,1)S(1)} %add_dynamic-update-slice_fusion.3), channel_id=1, source_target_pairs={{0,8},{1,9},{2,10},{3,11},{4,12},{5,13},{6,14},{7,15},{8,16},{9,17... | collective-permute-start | bytes 6291464 | tf_op jit(solution)/shard_map/ppermute | solution.py:38
  50.2 42.9 %collective-permute-start.27 = (bf16[1024,1024]{1,0:T(8,128)(2,1)S(1)}, bf16[1024,1024]{1,0:T(8,128)(2,1)S(1)}, u32[]{:S(2)}, u32[]{:S(2)}) collective-permute-start(bf16[1024,1024]{1,0:T(8,128)(2,1)S(1)} %add_dynamic-update-slice_fusion.2), channel_id=1, source_target_pairs={{0,24},{1,25},{2,26},{3,27},{4,28},{5,29},{6,30},{7,31},{8,0},{9,1... | collective-permute-start | bytes 6291464 | tf_op jit(solution)/shard_map/ppermute | solution.py:38
  53.4 3.5 %copy-start.8 = (f32[1,256,1024]{2,1,0:T(8,128)S(1)}, f32[1,256,1024]{2,1,0:T(8,128)}, u32[]{:S(2)}) copy-start(f32[1,256,1024]{2,1,0:T(8,128)} %w_ref.1) | copy-start | bytes 3145732
  53.4 59.5 %collective-permute-start.32 = (bf16[1024,1024]{1,0:T(8,128)(2,1)S(1)}, bf16[1024,1024]{1,0:T(8,128)(2,1)S(1)}, u32[]{:S(2)}, u32[]{:S(2)}) collective-permute-start(bf16[1024,1024]{1,0:T(8,128)(2,1)S(1)} %add_dynamic-update-slice_fusion.1), channel_id=1, source_target_pairs={{0,2},{1,3},{2,4},{3,5},{4,6},{5,7},{6,0},{7,1},{8,10},{9,11},{10,... | collective-permute-start | bytes 6291464 | tf_op jit(solution)/shard_map/ppermute | solution.py:38
  54.1 60.4 %collective-permute-start.34 = (bf16[1024,1024]{1,0:T(8,128)(2,1)S(1)}, bf16[1024,1024]{1,0:T(8,128)(2,1)S(1)}, u32[]{:S(2)}, u32[]{:S(2)}) collective-permute-start(bf16[1024,1024]{1,0:T(8,128)(2,1)S(1)} %add_dynamic-update-slice_fusion), channel_id=1, source_target_pairs={{0,6},{1,7},{2,0},{3,1},{4,2},{5,3},{6,4},{7,5},{8,14},{9,15},{10,... | collective-permute-start | bytes 6291464 | tf_op jit(solution)/shard_map/ppermute | solution.py:38
  57.1 47.7 %collective-permute-start.11 = (bf16[256,1024]{1,0:T(8,128)(2,1)S(1)}, bf16[256,1024]{1,0:T(8,128)(2,1)S(1)}, u32[]{:S(2)}, u32[]{:S(2)}) collective-permute-start(bf16[256,1024]{1,0:T(8,128)(2,1)S(1)} %convert_bitcast_fusion), channel_id=1, source_target_pairs={{0,16},{1,5},{2,18},{3,7},{4,20},{5,1},{6,22},{7,3},{8,24},{9,13},... | collective-permute-start | bytes 1572872 | tf_op jit(solution)/shard_map/ppermute | solution.py:55
  93.1 19.2 %collective-permute-start.12 = (bf16[256,1024]{1,0:T(8,128)(2,1)S(1)}, bf16[256,1024]{1,0:T(8,128)(2,1)S(1)}, u32[]{:S(2)}, u32[]{:S(2)}) collective-permute-start(bf16[256,1024]{1,0:T(8,128)(2,1)S(1)} %convert_bitcast_fusion), channel_id=1, source_target_pairs={{0,8},{1,3},{2,10},{3,5},{4,12},{5,7},{6,14},{7,1},{8,16},{9,11},{... | collective-permute-start | bytes 1572872 | tf_op jit(solution)/shard_map/ppermute | solution.py:55
  93.1 22.8 %collective-permute-start.7 = (bf16[256,1024]{1,0:T(8,128)(2,1)S(1)}, bf16[256,1024]{1,0:T(8,128)(2,1)S(1)}, u32[]{:S(2)}, u32[]{:S(2)}) collective-permute-start(bf16[256,1024]{1,0:T(8,128)(2,1)S(1)} %convert_bitcast_fusion), channel_id=1, source_target_pairs={{0,24},{1,7},{2,26},{3,1},{4,28},{5,3},{6,30},{7,5},{8,0},{9,15},{... | collective-permute-start | bytes 1572872 | tf_op jit(solution)/shard_map/ppermute | solution.py:55
  104.8 18.7 %collective-permute-start.28 = (bf16[1024,256]{1,0:T(8,128)(2,1)S(1)}, bf16[1024,256]{1,0:T(8,128)(2,1)S(1)}, u32[]{:S(2)}, u32[]{:S(2)}) collective-permute-start(bf16[1024,256]{1,0:T(8,128)(2,1)S(1)} %get-tuple-element.92), channel_id=1, source_target_pairs={{0,2},{1,3},{2,4},{3,5},{4,6},{5,7},{6,0},{7,1},{8,10},{9,11},{10,... | collective-permute-start | bytes 1572872 | tf_op jit(solution)/shard_map/ppermute | solution.py:38
  112.3 23.0 %collective-permute-start.29 = (bf16[1024,256]{1,0:T(8,128)(2,1)S(1)}, bf16[1024,256]{1,0:T(8,128)(2,1)S(1)}, u32[]{:S(2)}, u32[]{:S(2)}) collective-permute-start(bf16[1024,256]{1,0:T(8,128)(2,1)S(1)} %get-tuple-element.91), channel_id=1, source_target_pairs={{0,4},{1,5},{2,6},{3,7},{4,0},{5,1},{6,2},{7,3},{8,12},{9,13},{10,... | collective-permute-start | bytes 1572872 | tf_op jit(solution)/shard_map/ppermute | solution.py:38
  113.0 39.9 %collective-permute-start.13 = (bf16[512,1024]{1,0:T(8,128)(2,1)S(1)}, bf16[512,1024]{1,0:T(8,128)(2,1)S(1)}, u32[]{:S(2)}, u32[]{:S(2)}) collective-permute-start(bf16[512,1024]{1,0:T(8,128)(2,1)S(1)} %constant_dynamic-update-slice_fusion.rest_1_), channel_id=1, source_target_pairs={{0,1},{1,0},{2,3},{3,2},{4,5},{5,4},{6,7},{7,6},{8,9},{9,8},{10,11... | collective-permute-start | bytes 3145736 | tf_op jit(solution)/shard_map/ppermute | solution.py:38
  114.5 21.1 %collective-permute-start.30 = (bf16[1024,256]{1,0:T(8,128)(2,1)S(1)}, bf16[1024,256]{1,0:T(8,128)(2,1)S(1)}, u32[]{:S(2)}, u32[]{:S(2)}) collective-permute-start(bf16[1024,256]{1,0:T(8,128)(2,1)S(1)} %get-tuple-element.90), channel_id=1, source_target_pairs={{0,6},{1,7},{2,0},{3,1},{4,2},{5,3},{6,4},{7,5},{8,14},{9,15},{10,... | collective-permute-start | bytes 1572872 | tf_op jit(solution)/shard_map/ppermute | solution.py:38
  115.9 20.3 %collective-permute-start.35 = (bf16[1024,256]{1,0:T(8,128)(2,1)S(1)}, bf16[1024,256]{1,0:T(8,128)(2,1)S(1)}, u32[]{:S(2)}, u32[]{:S(2)}) collective-permute-start(bf16[1024,256]{1,0:T(8,128)(2,1)S(1)} %get-tuple-element.88), channel_id=1, source_target_pairs={{0,8},{1,9},{2,10},{3,11},{4,12},{5,13},{6,14},{7,15},{8,16},{9,17... | collective-permute-start | bytes 1572872 | tf_op jit(solution)/shard_map/ppermute | solution.py:38
  123.5 13.7 %collective-permute-start.36 = (bf16[1024,256]{1,0:T(8,128)(2,1)S(1)}, bf16[1024,256]{1,0:T(8,128)(2,1)S(1)}, u32[]{:S(2)}, u32[]{:S(2)}) collective-permute-start(bf16[1024,256]{1,0:T(8,128)(2,1)S(1)} %get-tuple-element.87), channel_id=1, source_target_pairs={{0,16},{1,17},{2,18},{3,19},{4,20},{5,21},{6,22},{7,23},{8,24},{9,... | collective-permute-start | bytes 1572872 | tf_op jit(solution)/shard_map/ppermute | solution.py:38
  135.3 15.5 %collective-permute-start.37 = (bf16[1024,256]{1,0:T(8,128)(2,1)S(1)}, bf16[1024,256]{1,0:T(8,128)(2,1)S(1)}, u32[]{:S(2)}, u32[]{:S(2)}) collective-permute-start(bf16[1024,256]{1,0:T(8,128)(2,1)S(1)} %get-tuple-element.86), channel_id=1, source_target_pairs={{0,24},{1,25},{2,26},{3,27},{4,28},{5,29},{6,30},{7,31},{8,0},{9,1... | collective-permute-start | bytes 1572872 | tf_op jit(solution)/shard_map/ppermute | solution.py:38
  135.6 44.2 %collective-permute-start.20 = (bf16[512,1024]{1,0:T(8,128)(2,1)S(1)}, bf16[512,1024]{1,0:T(8,128)(2,1)}, u32[]{:S(2)}, u32[]{:S(2)}) collective-permute-start(bf16[512,1024]{1,0:T(8,128)(2,1)S(1)} %constant_dynamic-update-slice_fusion.rest_1_), channel_id=1, source_target_pairs={{0,6},{1,25},{2,0},{3,27},{4,2},{5,29},{6,4},{7,31},{8,14},{9,1},{... | collective-permute-start | bytes 3145736 | tf_op jit(solution)/shard_map/ppermute | solution.py:55
  136.2 53.7 %collective-permute-start.22 = (bf16[512,1024]{1,0:T(8,128)(2,1)S(1)}, bf16[512,1024]{1,0:T(8,128)(2,1)}, u32[]{:S(2)}, u32[]{:S(2)}) collective-permute-start(bf16[512,1024]{1,0:T(8,128)(2,1)S(1)} %pad_maximum_fusion.rest_0_), channel_id=1, source_target_pairs={{0,2},{1,9},{2,4},{3,11},{4,6},{5,13},{6,0},{7,15},{8,10},{9,17},{... | collective-permute-start | bytes 3145736 | tf_op jit(solution)/shard_map/ppermute | solution.py:55
  137.2 52.8 %collective-permute-start.8 = (bf16[512,1024]{1,0:T(8,128)(2,1)S(1)}, bf16[512,1024]{1,0:T(8,128)(2,1)}, u32[]{:S(2)}, u32[]{:S(2)}) collective-permute-start(bf16[512,1024]{1,0:T(8,128)(2,1)S(1)} %pad_maximum_fusion.rest_0_), channel_id=1, source_target_pairs={{0,1},{1,0},{2,3},{3,2},{4,5},{5,4},{6,7},{7,6},{8,9},{9,8},{10,11... | collective-permute-start | bytes 3145736 | tf_op jit(solution)/shard_map/ppermute | solution.py:38
  150.8 39.6 %collective-permute-start.18 = (bf16[512,1024]{1,0:T(8,128)(2,1)S(1)}, bf16[512,1024]{1,0:T(8,128)(2,1)}, u32[]{:S(2)}, u32[]{:S(2)}) collective-permute-start(bf16[512,1024]{1,0:T(8,128)(2,1)S(1)} %constant_dynamic-update-slice_fusion.rest_1_), channel_id=1, source_target_pairs={{0,2},{1,9},{2,4},{3,11},{4,6},{5,13},{6,0},{7,15},{8,10},{9,17},{... | collective-permute-start | bytes 3145736 | tf_op jit(solution)/shard_map/ppermute | solution.py:55
  152.0 0.8 copy-start.3
  152.8 1.0 copy-start.1
  152.8 15.1 %collective-permute-start.38 = (bf16[1024,256]{1,0:T(8,128)(2,1)S(1)}, bf16[1024,256]{1,0:T(8,128)(2,1)S(1)}, u32[]{:S(2)}, u32[]{:S(2)}) collective-permute-start(bf16[1024,256]{1,0:T(8,128)(2,1)S(1)} %get-tuple-element.81), channel_id=1, source_target_pairs={{0,1},{1,0},{2,3},{3,2},{4,5},{5,4},{6,7},{7,6},{8,9},{9,8},{10,11... | collective-permute-start | bytes 1572872 | tf_op jit(solution)/shard_map/ppermute | solution.py:38
  168.0 0.8 copy-start.10
  168.8 26.9 %collective-permute-start.16 = (bf16[512,1024]{1,0:T(8,128)(2,1)S(1)}, bf16[512,1024]{1,0:T(8,128)(2,1)}, u32[]{:S(2)}, u32[]{:S(2)}) collective-permute-start(bf16[512,1024]{1,0:T(8,128)(2,1)S(1)} %pad_maximum_fusion.rest_0_), channel_id=1, source_target_pairs={{0,6},{1,25},{2,0},{3,27},{4,2},{5,29},{6,4},{7,31},{8,14},{9,1},{... | collective-permute-start | bytes 3145736 | tf_op jit(solution)/shard_map/ppermute | solution.py:55
  172.1 1.0 copy-start.4
  173.1 16.9 %copy-start.2 = (bf16[512,1024]{1,0:T(8,128)(2,1)S(1)}, bf16[512,1024]{1,0:T(8,128)(2,1)}, u32[]{:S(2)}) copy-start(bf16[512,1024]{1,0:T(8,128)(2,1)} %copy-done.1) | copy-start | bytes 3145732
  179.8 12.9 %collective-permute-start.39 = (f32[128,1024]{1,0:T(8,128)S(1)}, f32[128,1024]{1,0:T(8,128)S(1)}, u32[]{:S(2)}, u32[]{:S(2)}) collective-permute-start(f32[128,1024]{1,0:T(8,128)S(1)} %slice_select_fusion), channel_id=1, source_target_pairs={{0,32},{32,0},{64,96},{96,64},{1,33},{33,1},{65,97},{97,65},{2,34}... | collective-permute-start | bytes 1572872 | tf_op jit(solution)/shard_map/ppermute | solution.py:67
  189.9 26.3 %collective-permute-start.21 = (bf16[512,1024]{1,0:T(8,128)(2,1)}, bf16[512,1024]{1,0:T(8,128)(2,1)S(1)}, u32[]{:S(2)}, u32[]{:S(2)}) collective-permute-start(bf16[512,1024]{1,0:T(8,128)(2,1)} %collective-permute-done.20.rest_4_), channel_id=1, source_target_pairs={{0,1},{1,0},{2,3},{3,2},{4,5},{5,4},{6,7},{7,6},{8,9},{9,8},{10,11... | collective-permute-start | bytes 3145736 | tf_op jit(solution)/shard_map/ppermute | solution.py:38
  190.0 26.2 %collective-permute-start.14 = (bf16[512,1024]{1,0:T(8,128)(2,1)S(1)}, bf16[512,1024]{1,0:T(8,128)(2,1)S(1)}, u32[]{:S(2)}, u32[]{:S(2)}) collective-permute-start(bf16[512,1024]{1,0:T(8,128)(2,1)S(1)} %copy-done.2), channel_id=1, source_target_pairs={{0,8},{1,3},{2,10},{3,5},{4,12},{5,7},{6,14},{7,1},{8,16},{9,11},{... | collective-permute-start | bytes 3145736 | tf_op jit(solution)/shard_map/ppermute | solution.py:55
  190.4 28.5 %collective-permute-start.9 = (bf16[512,1024]{1,0:T(8,128)(2,1)}, bf16[512,1024]{1,0:T(8,128)(2,1)S(1)}, u32[]{:S(2)}, u32[]{:S(2)}) collective-permute-start(bf16[512,1024]{1,0:T(8,128)(2,1)} %collective-permute-done.8.rest_2_), channel_id=1, source_target_pairs={{0,24},{1,7},{2,26},{3,1},{4,28},{5,3},{6,30},{7,5},{8,0},{9,15},{... | collective-permute-start | bytes 3145736 | tf_op jit(solution)/shard_map/ppermute | solution.py:55
  192.7 57.9 %collective-permute-start.23 = (bf16[512,1024]{1,0:T(8,128)(2,1)}, bf16[512,1024]{1,0:T(8,128)(2,1)S(1)}, u32[]{:S(2)}, u32[]{:S(2)}) collective-permute-start(bf16[512,1024]{1,0:T(8,128)(2,1)} %collective-permute-done.22.rest_5_), channel_id=1, source_target_pairs={{0,1},{1,0},{2,3},{3,2},{4,5},{5,4},{6,7},{7,6},{8,9},{9,8},{10,11... | collective-permute-start | bytes 3145736 | tf_op jit(solution)/shard_map/ppermute | solution.py:38
  195.7 52.3 %collective-permute-start.40 = (f32[128,1024]{1,0:T(8,128)S(1)}, f32[128,1024]{1,0:T(8,128)S(1)}, u32[]{:S(2)}, u32[]{:S(2)}) collective-permute-start(f32[128,1024]{1,0:T(8,128)S(1)} %select_add_fusion), channel_id=1, source_target_pairs={{0,64},{32,96},{64,0},{96,32},{1,65},{33,97},{65,1},{97,33},{2,66}... | collective-permute-start | bytes 1572872 | tf_op jit(solution)/shard_map/ppermute | solution.py:67
  216.3 53.3 %collective-permute-start.19 = (bf16[512,1024]{1,0:T(8,128)(2,1)}, bf16[512,1024]{1,0:T(8,128)(2,1)S(1)}, u32[]{:S(2)}, u32[]{:S(2)}) collective-permute-start(bf16[512,1024]{1,0:T(8,128)(2,1)} %collective-permute-done.18.rest_1_), channel_id=1, source_target_pairs={{0,2},{1,9},{2,4},{3,11},{4,6},{5,13},{6,0},{7,15},{8,10},{9,17},{... | collective-permute-start | bytes 3145736 | tf_op jit(solution)/shard_map/ppermute | solution.py:55
  216.3 53.3 %collective-permute-start.17 = (bf16[512,1024]{1,0:T(8,128)(2,1)}, bf16[512,1024]{1,0:T(8,128)(2,1)S(1)}, u32[]{:S(2)}, u32[]{:S(2)}) collective-permute-start(bf16[512,1024]{1,0:T(8,128)(2,1)} %collective-permute-done.16.rest_0_), channel_id=1, source_target_pairs={{0,6},{1,25},{2,0},{3,27},{4,2},{5,29},{6,4},{7,31},{8,14},{9,1},{... | collective-permute-start | bytes 3145736 | tf_op jit(solution)/shard_map/ppermute | solution.py:55
  218.9 56.5 %collective-permute-start.15 = (bf16[512,1024]{1,0:T(8,128)(2,1)S(1)}, bf16[512,1024]{1,0:T(8,128)(2,1)S(1)}, u32[]{:S(2)}, u32[]{:S(2)}) collective-permute-start(bf16[512,1024]{1,0:T(8,128)(2,1)S(1)} %collective-permute-done.14.rest_1_), channel_id=1, source_target_pairs={{0,8},{1,3},{2,10},{3,5},{4,12},{5,7},{6,14},{7,1},{8,16},{9,11},{... | collective-permute-start | bytes 3145736 | tf_op jit(solution)/shard_map/ppermute | solution.py:55
  248.0 27.5 %collective-permute-start.10 = (bf16[512,1024]{1,0:T(8,128)(2,1)S(1)}, bf16[512,1024]{1,0:T(8,128)(2,1)S(1)}, u32[]{:S(2)}, u32[]{:S(2)}) collective-permute-start(bf16[512,1024]{1,0:T(8,128)(2,1)S(1)} %collective-permute-done.9.rest_0_), channel_id=1, source_target_pairs={{0,24},{1,7},{2,26},{3,1},{4,28},{5,3},{6,30},{7,5},{8,0},{9,15},{... | collective-permute-start | bytes 3145736 | tf_op jit(solution)/shard_map/ppermute | solution.py:55
  250.6 28.3 %collective-permute-start.41 = (f32[128,1024]{1,0:T(8,128)S(1)}, f32[128,1024]{1,0:T(8,128)S(1)}, u32[]{:S(2)}, u32[]{:S(2)}) collective-permute-start(f32[128,1024]{1,0:T(8,128)S(1)} %add.896), channel_id=1, source_target_pairs={{0,32},{32,0},{64,96},{96,64},{1,33},{33,1},{65,97},{97,65},{2,34}... | collective-permute-start | bytes 1572872 | tf_op jit(solution)/shard_map/ppermute | solution.py:67
  278.9 1.2 copy-start.7
  278.9 1.5 copy-start.9
where the time goes:
time: 283 us; the launch traced here: 282 us
  waiting for transfers between devices  143 us (51%)
  starting transfers between devices  67.1 us (24%)
  Pallas kernels  56.2 us (20%)
  local copies, waits for them, and re-layouts  8.4 us (3%)
  other arithmetic  6.4 us (2%)
    ppermute x26, waiting for transfers between devices, send(): return lax.ppermute(value, 'fsdp', pairs)  100 us
    ppermute x26, starting transfers between devices, send(): return lax.ppermute(value, 'fsdp', pairs)  39.1 us
    ppermute x3, waiting for transfers between devices, swap_rep(): return lax.ppermute(value, 'rep', [(r, r ^ bit) for r in range(4)])  28.6 us
    pallas_call x4, Pallas kernels, input_grad_part(): pl.pallas_call(functools.partial(input_grad_kernel, tuple(edges)), out_sh...  27.9 us
    pallas_call x2, Pallas kernels, products(): pl.pallas_call(kernel, out_shape=(jax.ShapeDtypeStruct((rows, 4 * SHARD),...  20.3 us
    ppermute x13, starting transfers between devices, send_tilted(): return lax.ppermute(value, ('rep', 'fsdp'), pairs)  16.5 us
    ppermute x13, waiting for transfers between devices, send_tilted(): return lax.ppermute(value, ('rep', 'fsdp'), pairs)  14.1 us
    ppermute x3, starting transfers between devices, swap_rep(): return lax.ppermute(value, 'rep', [(r, r ^ bit) for r in range(4)])  11.4 us
  transfers between devices with their start and end apart: 42, of which 12 were waited for; matrix products, arithmetic and copies ran while one was open for 2% of the time, Pallas kernels for 18%

commit v1 on v0

--- a/solution.py
+++ b/solution.py
@@ -115,11 +115,11 @@
         other = jnp.sum(jnp.where(row_col == seq - HALF, push, 0.0), axis=0, keepdims=True)
         weights.append(jnp.where(seq < HALF, -dpo_beta * chosen, dpo_beta * other))
     tok = lax.broadcasted_iota(jnp.int32, (1, ROWS), 1)
-    wrow = jnp.where(tok < SEQLEN, weights[0], weights[1]) * mrow_ref[...]
+    wrow = jnp.where(tok < SEQLEN, weights[0], weights[1]) * mrow_ref[...].astype(jnp.float32)
     cott_ref[...] = (wrow * tgt_ref[...].astype(jnp.float32)).astype(jnp.bfloat16)
     for i in range(SEQ_DEV):
         part = slice(i * SEQLEN, (i + 1) * SEQLEN)
-        wcol = weights[i] * mcol_ref[part, :]
+        wcol = weights[i] * mcol_ref[part, :].astype(jnp.float32)
         cot_ref[part, :] = (wcol * tg_ref[part, :].astype(jnp.float32)).astype(jnp.bfloat16)
 
 
@@ -266,7 +266,7 @@
 
 
 def adam(keep, recv, m, v, w, anchor):
-    col = 128
+    col = 256
     gt = pl.BlockSpec((col, SHARD), lambda j: (j, 0))
     cube = pl.BlockSpec((1, SHARD, col), lambda j: (0, 0, j))
     flat = pl.BlockSpec((SHARD, col), lambda j: (0, j))
@@ -313,7 +313,8 @@
     every, low, high = range(4), (0, 1), (2, 3)
     for group in (
         [("own", 0, every), ("oth", 0, every), ("own", 1, high), ("own", 3, low)],
-        [("own", 1, low), ("own", 3, high), ("oth", 1, high), ("oth", 3, low)],
+        [("own", 1, low), ("own", 3, high)],
+        [("oth", 1, high), ("oth", 3, low)],
         [("oth", 1, low), ("oth", 3, high), ("own", 2, every)],
         [("oth", 2, every)],
     ):
@@ -322,9 +323,8 @@
             entries = entries + gathered(*entry)
     tab = jnp.stack(entries).astype(jnp.int32)
 
-    mask_f = loss_mask.astype(f32)
     where_f = f.reshape(1).astype(jnp.int32)
-    row = seq_sums(where_f, log_ratio.reshape(ROWS // 128, 128), loss_mask.reshape(ROWS // 128, 128))
+    row = seq_sums(where_f, in_hbm(log_ratio.reshape(ROWS // 128, 128)), in_hbm(loss_mask.reshape(ROWS // 128, 128)))
     row = row + shift(row, dy=1)
     row = row + shift(row, dx=1) + shift(row, dx=-1) + shift(row, dx=2)
     rows = (row, shift(row, dz=1), shift(row, dz=-1), shift(row, dz=2))
@@ -343,7 +343,7 @@
 
     pairs_pad = jnp.pad(pairs, ((0, 0), (0, 128 - HALF)), constant_values=-1)
     cot, cott = make_cot(
-        where_f, rows, pairs_pad, mask_f.reshape(1, ROWS), mask_f.reshape(ROWS, 1),
+        where_f, rows, pairs_pad, loss_mask.reshape(1, ROWS), loss_mask.reshape(ROWS, 1),
         tok_grads, tok_grads.T,
     )
 
@@ -376,7 +376,7 @@
         sums += [parts[0]] + moved
     keep, give = choose(my.reshape(1).astype(jnp.int32), sums)
     recv = in_hbm(shift(in_hbm(give), dy=1))
-    new_m, delta = adam(keep, recv, in_hbm(adam_m), in_hbm(adam_v), in_hbm(inner_w), in_hbm(anchor))
+    new_m, delta = adam(in_hbm(keep), recv, in_hbm(adam_m), in_hbm(adam_v), in_hbm(inner_w), in_hbm(anchor))
 
     hs = SHARD // 2
     part = jnp.where(core == 0, delta[:hs], delta[hs:])
@@ -384,14 +384,16 @@
     part = part + swap_rep(other, 1)
     part = part + swap_rep(part, 2)
     other = swap_rep(part, 1)
-    total = jnp.concatenate([jnp.where(core == 0, part, other), jnp.where(core == 0, other, part)], axis=0)
+    swapped = core == 1
+    total = jnp.concatenate([jnp.where(swapped, other, part), jnp.where(swapped, part, other)], axis=0)
     delta_avg = total / 4
     new_mom = momentum * outer_mom + delta_avg
     new_anchor = anchor - outer_rate * (delta_avg + momentum * new_mom)
 
     groups = (
         (row_low, row_high, other_low, other_high, next_high, prev_low),
-        (next_low, prev_high) + rest,
+        (next_low, prev_high),
+        rest,
         cross + relay,
         last,
     )

time: 283 us -> 289 us (1.021)
  Pallas kernels: 56.2 us -> 62.4 us
    pallas_call x4 -> x5, Pallas kernels: 27.9 us -> 35.2 us  [input_grad_part(): pl.pallas_call(functools.partial(input_grad_kernel, tuple(edges)), out_sh...]
    unnamed x26 -> x32, local copies, waits for them, and re-layouts: 8.03 us -> 7.3 us
  transfers between devices with their start and end apart: 42 -> 42, of which waited for: 12 -> 13; matrix products, arithmetic and copies ran while one was open for 2% -> 2% of each run, Pallas kernels for 18% -> 19%
where the time goes in v1:
time: 289 us; the launch traced here: 288 us
  waiting for transfers between devices  142 us (49%)
  starting transfers between devices  68.2 us (24%)
  Pallas kernels  62.4 us (22%)
  local copies, waits for them, and re-layouts  7.67 us (3%)
  other arithmetic  7.04 us (2%)
    ppermute x26, waiting for transfers between devices, send(): return lax.ppermute(value, 'fsdp', pairs)  99.8 us
    ppermute x26, starting transfers between devices, send(): return lax.ppermute(value, 'fsdp', pairs)  40 us
    pallas_call x5, Pallas kernels, input_grad_part(): pl.pallas_call(functools.partial(input_grad_kernel, tuple(edges)), out_sh...  35.2 us
    ppermute x3, waiting for transfers between devices, swap_rep(): return lax.ppermute(value, 'rep', [(r, r ^ bit) for r in range(4)])  28 us
    pallas_call x2, Pallas kernels, products(): pl.pallas_call(kernel, out_shape=(jax.ShapeDtypeStruct((rows, 4 * SHARD),...  20.3 us
    ppermute x13, starting transfers between devices, send_tilted(): return lax.ppermute(value, ('rep', 'fsdp'), pairs)  16 us
    ppermute x13, waiting for transfers between devices, send_tilted(): return lax.ppermute(value, ('rep', 'fsdp'), pairs)  14.2 us
    ppermute x3, starting transfers between devices, swap_rep(): return lax.ppermute(value, 'rep', [(r, r ^ bit) for r in range(4)])  12.3 us
  transfers between devices with their start and end apart: 42, of which 13 were waited for; matrix products, arithmetic and copies ran while one was open for 2% of the time, Pallas kernels for 19%

profile of v1, /device:TPU:1, one launch (start us, length us, event | category | flops | bytes accessed | tf_op | source)
XLA Modules:
  0.0 288.4 jit_solution(1199609238003532772)
XLA Ops:
  0.7 0.9 seq_sums.1
  1.5 3.7 %collective-permute-start = (f32[1,128]{1,0:T(1,128)S(1)}, f32[1,128]{1,0:T(1,128)S(1)}, u32[]{:S(2)}, u32[]{:S(2)}) collective-permute-start(f32[1,128]{1,0:T(1,128)S(1)} %seq_sums.1), channel_id=1, source_target_pairs={{0,1},{1,0},{2,3},{3,2},{4,5},{5,4},{6,7},{7,6},{8,9},{9,8},{10,11... | collective-permute-start | bytes 1544 | tf_op jit(solution)/shard_map/ppermute | solution.py:38
  5.3 1.0 collective-permute-done
  6.2 1.3 collective-permute-start.1
  7.5 1.4 collective-permute-start.2
  8.9 1.6 collective-permute-start.3
  10.5 1.5 copy.19
  12.2 0.6 collective-permute-done.3
  12.9 1.7 collective-permute-start.4
  14.5 2.2 collective-permute-start.5
  16.7 1.2 collective-permute-start.6
  18.2 2.5 collective-permute-done.6.v3_ref
  20.7 0.7 make_cot.1
  21.4 5.7 %shard_map.130 = (bf16[512,1024]{1,0:T(8,128)(2,1)S(1)}, bf16[512,1024]{1,0:T(8,128)(2,1)S(1)}, bf16[512,1024]{1,0:T(8,128)(2,1)S(1)}, bf16[512,1024]{1,0:T(8,128)(2,1)S(1)}) custom-call(s32[64]{0:T(128)S(1)} %stack.259.tab, bf16[1024,512]{1,0:T(8,128)(2,1)S(1)} %get-tuple-element.69.cott_ref, bf16[512,8192]{1,0:T(8,128)(2,1)} %a1.3, bf16[512,8192]{1,0:T(8,128)(2,1)} %a1.3), custom_call_target="tpu_custom_call" | custom-call | flops 2147483648 | bytes 6291456 | tf_op jit(solution)/shard_map/pallas_call | solution.py:170
  27.2 2.7 collective-permute-start.26
  29.9 2.7 collective-permute-start.33
  32.6 14.6 %shard_map.129 = (bf16[1024,1024]{1,0:T(8,128)(2,1)S(1)}, bf16[1024,1024]{1,0:T(8,128)(2,1)S(1)}, bf16[1024,1024]{1,0:T(8,128)(2,1)S(1)}, bf16[1024,1024]{1,0:T(...) custom-call(s32[64]{0:T(128)S(1)} %stack.259.tab, ...), custom_call_target="tpu_custom_call" | custom-call | flops 6442450944 | bytes 18874368 | tf_op jit(solution)/shard_map/pallas_call | solution.py:170
  47.1 1.0 collective-permute-done.24
  49.4 2.7 collective-permute-start.27
  53.3 2.9 %collective-permute-start.34 = (bf16[1024,1024]{1,0:T(8,128)(2,1)S(1)}, bf16[1024,1024]{1,0:T(8,128)(2,1)S(1)}, u32[]{:S(2)}, u32[]{:S(2)}) collective-permute-start(bf16[1024,1024]{1,0:T(8,128)(2,1)S(1)} %add_dynamic-update-slice_fusion), channel_id=1, source_target_pairs={{0,6},{1,7},{2,0},{3,1},{4,2},{5,3},{6,4},{7,5},{8,14},{9,15},{10,... | collective-permute-start | bytes 6291464 | tf_op jit(solution)/shard_map/ppermute | solution.py:38
  56.4 35.9 %collective-permute-done.25 = bf16[1024,1024]{1,0:T(8,128)(2,1)S(1)} collective-permute-done((bf16[1024,1024]{1,0:T(8,128)(2,1)S(1)}, bf16[1024,1024]{1,0:T(8,128)(2,1)S(1)}, u32[]{:S(2)}, u32[]{:S(2)}) %collective-permute-start.25) | collective-permute-done | bytes 2097184 | tf_op jit(solution)/shard_map/ppermute | solution.py:38
  92.3 2.7 collective-permute-start.7
  94.9 0.7 add_convert_fusion.4
  95.7 8.3 %collective-permute-done.11 = bf16[256,1024]{1,0:T(8,128)(2,1)S(1)} collective-permute-done((bf16[256,1024]{1,0:T(8,128)(2,1)S(1)}, bf16[256,1024]{1,0:T(8,128)(2,1)S(1)}, u32[]{:S(2)}, u32[]{:S(2)}) %collective-permute-start.11) | collective-permute-done | bytes 524320 | tf_op jit(solution)/shard_map/ppermute | solution.py:55
  104.0 1.5 collective-permute-start.28
  105.5 5.9 %collective-permute-done.12 = bf16[256,1024]{1,0:T(8,128)(2,1)S(1)} collective-permute-done((bf16[256,1024]{1,0:T(8,128)(2,1)S(1)}, bf16[256,1024]{1,0:T(8,128)(2,1)S(1)}, u32[]{:S(2)}, u32[]{:S(2)}) %collective-permute-start.12) | collective-permute-done | bytes 524320 | tf_op jit(solution)/shard_map/ppermute | solution.py:55
  111.4 0.6 collective-permute-start.29
  112.1 1.7 collective-permute-start.13
  113.8 0.6 collective-permute-start.30
  114.4 0.7 add_convert_fusion
  115.2 7.4 %collective-permute-done.28.refs_1_ = bf16[1024,256]{1,0:T(8,128)(2,1)S(1)} collective-permute-done((bf16[1024,256]{1,0:T(8,128)(2,1)S(1)}, bf16[1024,256]{1,0:T(8,128)(2,1)S(1)}, u32[]{:S(2)}, u32[]{:S(2)}) %collective-permute-start.28) | collective-permute-done | bytes 524320 | tf_op jit(solution)/shard_map/ppermute | solution.py:38
  122.6 2.1 collective-permute-start.36
  124.7 9.8 %collective-permute-done.29.refs_2_ = bf16[1024,256]{1,0:T(8,128)(2,1)S(1)} collective-permute-done((bf16[1024,256]{1,0:T(8,128)(2,1)S(1)}, bf16[1024,256]{1,0:T(8,128)(2,1)S(1)}, u32[]{:S(2)}, u32[]{:S(2)}) %collective-permute-start.29) | collective-permute-done | bytes 524320 | tf_op jit(solution)/shard_map/ppermute | solution.py:38
  134.8 0.7 collective-permute-start.20
  135.6 0.8 collective-permute-start.22
  136.4 5.9 %collective-permute-start.8 = (bf16[512,1024]{1,0:T(8,128)(2,1)S(1)}, bf16[512,1024]{1,0:T(8,128)(2,1)}, u32[]{:S(2)}, u32[]{:S(2)}) collective-permute-start(bf16[512,1024]{1,0:T(8,128)(2,1)S(1)} %pad_maximum_fusion.rest_0_), channel_id=1, source_target_pairs={{0,1},{1,0},{2,3},{3,2},{4,5},{5,4},{6,7},{7,6},{8,9},{9,8},{10,11... | collective-permute-start | bytes 3145736 | tf_op jit(solution)/shard_map/ppermute | solution.py:38
  142.3 7.6 %collective-permute-done.37.refs_7_ = bf16[1024,256]{1,0:T(8,128)(2,1)S(1)} collective-permute-done((bf16[1024,256]{1,0:T(8,128)(2,1)S(1)}, bf16[1024,256]{1,0:T(8,128)(2,1)S(1)}, u32[]{:S(2)}, u32[]{:S(2)}) %collective-permute-start.37) | collective-permute-done | bytes 524320 | tf_op jit(solution)/shard_map/ppermute | solution.py:38
  149.9 0.6 choose.1
  150.5 0.8 copy-done.6
  151.3 1.0 copy-done.1
  152.3 14.3 %collective-permute-done.38.recv_ref = bf16[1024,256]{1,0:T(8,128)(2,1)S(1)} collective-permute-done((bf16[1024,256]{1,0:T(8,128)(2,1)S(1)}, bf16[1024,256]{1,0:T(8,128)(2,1)S(1)}, u32[]{:S(2)}, u32[]{:S(2)}) %collective-permute-start.38) | collective-permute-done | bytes 524320 | tf_op jit(solution)/shard_map/ppermute | solution.py:38
  166.6 0.8 copy-done.13
  167.4 3.8 %collective-permute-start.16 = (bf16[512,1024]{1,0:T(8,128)(2,1)S(1)}, bf16[512,1024]{1,0:T(8,128)(2,1)}, u32[]{:S(2)}, u32[]{:S(2)}) collective-permute-start(bf16[512,1024]{1,0:T(8,128)(2,1)S(1)} %pad_maximum_fusion.rest_0_), channel_id=1, source_target_pairs={{0,6},{1,25},{2,0},{3,27},{4,2},{5,29},{6,4},{7,31},{8,14},{9,1},{... | collective-permute-start | bytes 3145736 | tf_op jit(solution)/shard_map/ppermute | solution.py:55
  171.2 4.7 %adam.1 = (f32[1,256,1024]{2,1,0:T(8,128)}, f32[256,1024]{1,0:T(8,128)S(1)}) custom-call(bf16[1024,256]{1,0:T(8,128)(2,1)} %copy-done.6, bf16[1024,256]{1,0:T(8,128)(2,1)} %copy-done.13, f32[1,256,1024]{2,1,0:T(8,128)} %m_ref.1, f32[1,256,1024]{2,1,0:T(8,128)} %v_ref.1, f32[1,256,1024]{2,1,0:T(8,128)} %w_ref.1, f32[256,1024]{1,0:T(8,128)} %anchor_ref.1), custom_call_target="tpu_custom_call" | custom-call | flops 5242880 | bytes 7340032 | tf_op jit(solution)/shard_map/adam/pallas_call | solution.py:273
  175.9 10.2 %collective-permute-start.39 = (f32[128,1024]{1,0:T(8,128)S(1)}, f32[128,1024]{1,0:T(8,128)S(1)}, u32[]{:S(2)}, u32[]{:S(2)}) collective-permute-start(f32[128,1024]{1,0:T(8,128)S(1)} %slice_select_fusion), channel_id=1, source_target_pairs={{0,32},{32,0},{64,96},{96,64},{1,33},{33,1},{65,97},{97,65},{2,34}... | collective-permute-start | bytes 1572872 | tf_op jit(solution)/shard_map/ppermute | solution.py:67
  186.1 0.8 collective-permute-start.21
  186.9 2.7 collective-permute-start.9
  189.5 2.2 collective-permute-start.23
  191.9 0.9 collective-permute-start.40
  192.8 19.6 %collective-permute-done.21.rest_0_ = bf16[512,1024]{1,0:T(8,128)(2,1)S(1)} collective-permute-done((bf16[512,1024]{1,0:T(8,128)(2,1)}, bf16[512,1024]{1,0:T(8,128)(2,1)S(1)}, u32[]{:S(2)}, u32[]{:S(2)}) %collective-permute-start.21) | collective-permute-done | bytes 1048608 | tf_op jit(solution)/shard_map/ppermute | solution.py:38
  212.4 1.0 copy-done.4
  213.4 2.7 collective-permute-start.17
  216.1 28.0 %collective-permute-done.40 = f32[128,1024]{1,0:T(8,128)S(1)} collective-permute-done((f32[128,1024]{1,0:T(8,128)S(1)}, f32[128,1024]{1,0:T(8,128)S(1)}, u32[]{:S(2)}, u32[]{:S(2)}) %collective-permute-start.40) | collective-permute-done | bytes 524320 | tf_op jit(solution)/shard_map/ppermute | solution.py:67
  244.1 0.8 copy-done.12
  244.9 2.6 collective-permute-start.10
  247.5 1.3 add.896
  248.9 1.2 collective-permute-start.41
  250.0 11.0 %input_grad.5.rest_2_ = bf16[512,8192]{1,0:T(8,128)(2,1)} custom-call(s32[64]{0:T(128)S(1)} %stack.259.tab, bf16[512,1024]{1,0:T(8,128)(2,1)S(1)} %get-tuple-element.68.cot_ref, bf16[512,1024]{1,0:T(8,128)(2,1)S(1)} %pad_maximum_fusion.rest_0_, bf16[512,1024]{1,0:T(8,128)(2,1)S(1)} %constant_dynamic-update-slice_fusion.rest_1_, ...), custom_call_target="tpu_custom_call" | custom-call | flops 3221225472 | bytes 10485760 | tf_op jit(solution)/shard_map/input_grad/pallas_call | solution.py:209
  261.1 5.2 %input_grad.6.rest_2_ = bf16[512,8192]{1,0:T(8,128)(2,1)} custom-call(s32[64]{0:T(128)S(1)} %stack.259.tab, bf16[512,1024]{1,0:T(8,128)(2,1)S(1)} %get-tuple-element.68.cot_ref, bf16[512,1024]{1,0:T(8,128)(2,1)} %collective-permute-done.16.rest_0_, bf16[512,1024]{1,0:T(8,128)(2,1)} %collective-permute-done.18.rest_1_, ...), custom_call_target="tpu_custom_call", output_to_operand_aliasing={{}: (4, {})} | custom-call | flops 1073741824 | bytes 4194304 | tf_op jit(solution)/shard_map/input_grad/pallas_call | solution.py:209
  266.2 5.0 %input_grad.7.rest_4_ = bf16[512,8192]{1,0:T(8,128)(2,1)} custom-call(s32[64]{0:T(128)S(1)} %stack.259.tab, bf16[512,1024]{1,0:T(8,128)(2,1)S(1)} %get-tuple-element.68.cot_ref, bf16[512,1024]{1,0:T(8,128)(2,1)S(1)} %copy-done.5, bf16[512,1024]{1,0:T(8,128)(2,1)} %collective-permute-done.23.rest_1_, ...), custom_call_target="tpu_custom_call", output_to_operand_aliasing={{}: (4, {})} | custom-call | flops 1073741824 | bytes 4194304 | tf_op jit(solution)/shard_map/input_grad/pallas_call | solution.py:209
  271.2 8.8 %input_grad.8.rest_2_ = bf16[512,8192]{1,0:T(8,128)(2,1)} custom-call(s32[64]{0:T(128)S(1)} %stack.259.tab, bf16[512,1024]{1,0:T(8,128)(2,1)S(1)} %get-tuple-element.68.cot_ref, bf16[512,1024]{1,0:T(8,128)(2,1)} %collective-permute-done.9.rest_0_, bf16[512,1024]{1,0:T(8,128)(2,1)} %collective-permute-done.14.rest_1_, ...), custom_call_target="tpu_custom_call", output_to_operand_aliasing={{}: (6, {})} | custom-call | flops 2147483648 | bytes 7340032 | tf_op jit(solution)/shard_map/input_grad/pallas_call | solution.py:209
  280.1 5.2 %input_grad.9 = bf16[512,8192]{1,0:T(8,128)(2,1)} custom-call(s32[64]{0:T(128)S(1)} %stack.259.tab, bf16[512,1024]{1,0:T(8,128)(2,1)S(1)} %get-tuple-element.68.cot_ref, bf16[512,1024]{1,0:T(8,128)(2,1)} %collective-permute-done.10.rest_0_, bf16[512,1024]{1,0:T(8,128)(2,1)} %collective-permute-done.15.rest_1_, ...), custom_call_target="tpu_custom_call", output_to_operand_aliasing={{}: (4, {})} | custom-call | flops 1073741824 | bytes 4194304 | tf_op jit(solution)/shard_map/input_grad/pallas_call | solution.py:209
  285.3 1.1 copy-done.8
  286.8 1.7 multiply_subtract_fusion
  (82 shorter events, 4.1 us)
Async XLA Ops:
  0.6 11.4 %copy-start.7 = (s32[512]{0:T(512)S(1)}, s32[512]{0:T(512)}, u32[]{:S(2)}) copy-start(s32[512]{0:T(512)} %param.21) | copy-start | bytes 6148
  0.6 20.0 %copy-start = (bf16[512,1024]{1,0:T(8,128)(2,1)S(1)}, bf16[512,1024]{1,0:T(8,128)(2,1)}, u32[]{:S(2)}) copy-start(bf16[512,1024]{1,0:T(8,128)(2,1)} %tg_ref.1) | copy-start | bytes 3145732
  0.7 11.5 %copy-start.14 = (s32[1,32]{1,0:T(1,128)S(1)}, s32[1,32]{1,0:T(1,128)}, u32[]{:S(2)}) copy-start(s32[1,32]{1,0:T(1,128)} %param.22) | copy-start | bytes 388
  1.5 4.7 %collective-permute-start = (f32[1,128]{1,0:T(1,128)S(1)}, f32[1,128]{1,0:T(1,128)S(1)}, u32[]{:S(2)}, u32[]{:S(2)}) collective-permute-start(f32[1,128]{1,0:T(1,128)S(1)} %seq_sums.1), channel_id=1, source_target_pairs={{0,1},{1,0},{2,3},{3,2},{4,5},{5,4},{6,7},{7,6},{8,9},{9,8},{10,11... | collective-permute-start | bytes 1544 | tf_op jit(solution)/shard_map/ppermute | solution.py:38
  6.2 5.9 %collective-permute-start.1 = (f32[1,128]{1,0:T(1,128)S(1)}, f32[1,128]{1,0:T(1,128)S(1)}, u32[]{:S(2)}, u32[]{:S(2)}) collective-permute-start(f32[1,128]{1,0:T(1,128)S(1)} %add.871), channel_id=1, source_target_pairs={{0,8},{1,9},{2,10},{3,11},{4,12},{5,13},{6,14},{7,15},{8,16},{9,17... | collective-permute-start | bytes 1544 | tf_op jit(solution)/shard_map/ppermute | solution.py:38
  7.5 4.7 %collective-permute-start.2 = (f32[1,128]{1,0:T(1,128)S(1)}, f32[1,128]{1,0:T(1,128)S(1)}, u32[]{:S(2)}, u32[]{:S(2)}) collective-permute-start(f32[1,128]{1,0:T(1,128)S(1)} %add.871), channel_id=1, source_target_pairs={{0,24},{1,25},{2,26},{3,27},{4,28},{5,29},{6,30},{7,31},{8,0},{9,1... | collective-permute-start | bytes 1544 | tf_op jit(solution)/shard_map/ppermute | solution.py:38
  8.9 3.9 %collective-permute-start.3 = (f32[1,128]{1,0:T(1,128)S(1)}, f32[1,128]{1,0:T(1,128)S(1)}, u32[]{:S(2)}, u32[]{:S(2)}) collective-permute-start(f32[1,128]{1,0:T(1,128)S(1)} %add.871), channel_id=1, source_target_pairs={{0,16},{1,17},{2,18},{3,19},{4,20},{5,21},{6,22},{7,23},{8,24},{9,... | collective-permute-start | bytes 1544 | tf_op jit(solution)/shard_map/ppermute | solution.py:38
  12.9 5.3 %collective-permute-start.4 = (f32[1,128]{1,0:T(1,128)S(1)}, f32[1,128]{1,0:T(1,128)S(1)}, u32[]{:S(2)}, u32[]{:S(2)}) collective-permute-start(f32[1,128]{1,0:T(1,128)S(1)} %add_add_fusion.v0_ref), channel_id=1, source_target_pairs={{0,2},{1,3},{2,4},{3,5},{4,6},{5,7},{6,0},{7,1},{8,10},{9,11},{10,... | collective-permute-start | bytes 1544 | tf_op jit(solution)/shard_map/ppermute | solution.py:38
  14.5 3.6 %collective-permute-start.5 = (f32[1,128]{1,0:T(1,128)S(1)}, f32[1,128]{1,0:T(1,128)S(1)}, u32[]{:S(2)}, u32[]{:S(2)}) collective-permute-start(f32[1,128]{1,0:T(1,128)S(1)} %add_add_fusion.v0_ref), channel_id=1, source_target_pairs={{0,6},{1,7},{2,0},{3,1},{4,2},{5,3},{6,4},{7,5},{8,14},{9,15},{10,... | collective-permute-start | bytes 1544 | tf_op jit(solution)/shard_map/ppermute | solution.py:38
  16.7 3.9 %collective-permute-start.6 = (f32[1,128]{1,0:T(1,128)S(1)}, f32[1,128]{1,0:T(1,128)S(1)}, u32[]{:S(2)}, u32[]{:S(2)}) collective-permute-start(f32[1,128]{1,0:T(1,128)S(1)} %add_add_fusion.v0_ref), channel_id=1, source_target_pairs={{0,4},{1,5},{2,6},{3,7},{4,0},{5,1},{6,2},{7,3},{8,12},{9,13},{10,... | collective-permute-start | bytes 1544 | tf_op jit(solution)/shard_map/ppermute | solution.py:38
  27.1 21.0 %collective-permute-start.24 = (bf16[512,1024]{1,0:T(8,128)(2,1)S(1)}, bf16[512,1024]{1,0:T(8,128)(2,1)S(1)}, u32[]{:S(2)}, u32[]{:S(2)}) collective-permute-start(bf16[512,1024]{1,0:T(8,128)(2,1)S(1)} %get-tuple-element.72), channel_id=1, source_target_pairs={{0,8},{1,9},{2,10},{3,11},{4,12},{5,13},{6,14},{7,15},{8,16},{9,17... | collective-permute-start | bytes 3145736 | tf_op jit(solution)/shard_map/ppermute | solution.py:38
  27.2 21.6 %collective-permute-start.26 = (bf16[512,1024]{1,0:T(8,128)(2,1)S(1)}, bf16[512,1024]{1,0:T(8,128)(2,1)S(1)}, u32[]{:S(2)}, u32[]{:S(2)}) collective-permute-start(bf16[512,1024]{1,0:T(8,128)(2,1)S(1)} %get-tuple-element.74), channel_id=1, source_target_pairs={{0,24},{1,25},{2,26},{3,27},{4,28},{5,29},{6,30},{7,31},{8,0},{9,1... | collective-permute-start | bytes 3145736 | tf_op jit(solution)/shard_map/ppermute | solution.py:38
  29.9 22.2 %collective-permute-start.31 = (bf16[512,1024]{1,0:T(8,128)(2,1)S(1)}, bf16[512,1024]{1,0:T(8,128)(2,1)S(1)}, u32[]{:S(2)}, u32[]{:S(2)}) collective-permute-start(bf16[512,1024]{1,0:T(8,128)(2,1)S(1)} %get-tuple-element.77), channel_id=1, source_target_pairs={{0,2},{1,3},{2,4},{3,5},{4,6},{5,7},{6,0},{7,1},{8,10},{9,11},{10,... | collective-permute-start | bytes 3145736 | tf_op jit(solution)/shard_map/ppermute | solution.py:38
  29.9 22.8 %collective-permute-start.33 = (bf16[512,1024]{1,0:T(8,128)(2,1)S(1)}, bf16[512,1024]{1,0:T(8,128)(2,1)S(1)}, u32[]{:S(2)}, u32[]{:S(2)}) collective-permute-start(bf16[512,1024]{1,0:T(8,128)(2,1)S(1)} %get-tuple-element.79), channel_id=1, source_target_pairs={{0,6},{1,7},{2,0},{3,1},{4,2},{5,3},{6,4},{7,5},{8,14},{9,15},{10,... | collective-permute-start | bytes 3145736 | tf_op jit(solution)/shard_map/ppermute | solution.py:38
  48.7 43.5 %collective-permute-start.25 = (bf16[1024,1024]{1,0:T(8,128)(2,1)S(1)}, bf16[1024,1024]{1,0:T(8,128)(2,1)S(1)}, u32[]{:S(2)}, u32[]{:S(2)}) collective-permute-start(bf16[1024,1024]{1,0:T(8,128)(2,1)S(1)} %add_dynamic-update-slice_fusion.3), channel_id=1, source_target_pairs={{0,8},{1,9},{2,10},{3,11},{4,12},{5,13},{6,14},{7,15},{8,16},{9,17... | collective-permute-start | bytes 6291464 | tf_op jit(solution)/shard_map/ppermute | solution.py:38
  49.4 42.9 %collective-permute-start.27 = (bf16[1024,1024]{1,0:T(8,128)(2,1)S(1)}, bf16[1024,1024]{1,0:T(8,128)(2,1)S(1)}, u32[]{:S(2)}, u32[]{:S(2)}) collective-permute-start(bf16[1024,1024]{1,0:T(8,128)(2,1)S(1)} %add_dynamic-update-slice_fusion.2), channel_id=1, source_target_pairs={{0,24},{1,25},{2,26},{3,27},{4,28},{5,29},{6,30},{7,31},{8,0},{9,1... | collective-permute-start | bytes 6291464 | tf_op jit(solution)/shard_map/ppermute | solution.py:38
  52.6 3.6 %copy-start.9 = (f32[1,256,1024]{2,1,0:T(8,128)S(1)}, f32[1,256,1024]{2,1,0:T(8,128)}, u32[]{:S(2)}) copy-start(f32[1,256,1024]{2,1,0:T(8,128)} %w_ref.1) | copy-start | bytes 3145732
  52.6 59.4 %collective-permute-start.32 = (bf16[1024,1024]{1,0:T(8,128)(2,1)S(1)}, bf16[1024,1024]{1,0:T(8,128)(2,1)S(1)}, u32[]{:S(2)}, u32[]{:S(2)}) collective-permute-start(bf16[1024,1024]{1,0:T(8,128)(2,1)S(1)} %add_dynamic-update-slice_fusion.1), channel_id=1, source_target_pairs={{0,2},{1,3},{2,4},{3,5},{4,6},{5,7},{6,0},{7,1},{8,10},{9,11},{10,... | collective-permute-start | bytes 6291464 | tf_op jit(solution)/shard_map/ppermute | solution.py:38
  53.3 60.5 %collective-permute-start.34 = (bf16[1024,1024]{1,0:T(8,128)(2,1)S(1)}, bf16[1024,1024]{1,0:T(8,128)(2,1)S(1)}, u32[]{:S(2)}, u32[]{:S(2)}) collective-permute-start(bf16[1024,1024]{1,0:T(8,128)(2,1)S(1)} %add_dynamic-update-slice_fusion), channel_id=1, source_target_pairs={{0,6},{1,7},{2,0},{3,1},{4,2},{5,3},{6,4},{7,5},{8,14},{9,15},{10,... | collective-permute-start | bytes 6291464 | tf_op jit(solution)/shard_map/ppermute | solution.py:38
  56.3 47.7 %collective-permute-start.11 = (bf16[256,1024]{1,0:T(8,128)(2,1)S(1)}, bf16[256,1024]{1,0:T(8,128)(2,1)S(1)}, u32[]{:S(2)}, u32[]{:S(2)}) collective-permute-start(bf16[256,1024]{1,0:T(8,128)(2,1)S(1)} %convert_bitcast_fusion), channel_id=1, source_target_pairs={{0,16},{1,5},{2,18},{3,7},{4,20},{5,1},{6,22},{7,3},{8,24},{9,13},... | collective-permute-start | bytes 1572872 | tf_op jit(solution)/shard_map/ppermute | solution.py:55
  92.3 19.1 %collective-permute-start.12 = (bf16[256,1024]{1,0:T(8,128)(2,1)S(1)}, bf16[256,1024]{1,0:T(8,128)(2,1)S(1)}, u32[]{:S(2)}, u32[]{:S(2)}) collective-permute-start(bf16[256,1024]{1,0:T(8,128)(2,1)S(1)} %convert_bitcast_fusion), channel_id=1, source_target_pairs={{0,8},{1,3},{2,10},{3,5},{4,12},{5,7},{6,14},{7,1},{8,16},{9,11},{... | collective-permute-start | bytes 1572872 | tf_op jit(solution)/shard_map/ppermute | solution.py:55
  92.3 22.9 %collective-permute-start.7 = (bf16[256,1024]{1,0:T(8,128)(2,1)S(1)}, bf16[256,1024]{1,0:T(8,128)(2,1)S(1)}, u32[]{:S(2)}, u32[]{:S(2)}) collective-permute-start(bf16[256,1024]{1,0:T(8,128)(2,1)S(1)} %convert_bitcast_fusion), channel_id=1, source_target_pairs={{0,24},{1,7},{2,26},{3,1},{4,28},{5,3},{6,30},{7,5},{8,0},{9,15},{... | collective-permute-start | bytes 1572872 | tf_op jit(solution)/shard_map/ppermute | solution.py:55
  104.0 18.7 %collective-permute-start.28 = (bf16[1024,256]{1,0:T(8,128)(2,1)S(1)}, bf16[1024,256]{1,0:T(8,128)(2,1)S(1)}, u32[]{:S(2)}, u32[]{:S(2)}) collective-permute-start(bf16[1024,256]{1,0:T(8,128)(2,1)S(1)} %get-tuple-element.92), channel_id=1, source_target_pairs={{0,2},{1,3},{2,4},{3,5},{4,6},{5,7},{6,0},{7,1},{8,10},{9,11},{10,... | collective-permute-start | bytes 1572872 | tf_op jit(solution)/shard_map/ppermute | solution.py:38
  111.4 23.1 %collective-permute-start.29 = (bf16[1024,256]{1,0:T(8,128)(2,1)S(1)}, bf16[1024,256]{1,0:T(8,128)(2,1)S(1)}, u32[]{:S(2)}, u32[]{:S(2)}) collective-permute-start(bf16[1024,256]{1,0:T(8,128)(2,1)S(1)} %get-tuple-element.91), channel_id=1, source_target_pairs={{0,4},{1,5},{2,6},{3,7},{4,0},{5,1},{6,2},{7,3},{8,12},{9,13},{10,... | collective-permute-start | bytes 1572872 | tf_op jit(solution)/shard_map/ppermute | solution.py:38
  112.1 39.2 %collective-permute-start.13 = (bf16[512,1024]{1,0:T(8,128)(2,1)S(1)}, bf16[512,1024]{1,0:T(8,128)(2,1)S(1)}, u32[]{:S(2)}, u32[]{:S(2)}) collective-permute-start(bf16[512,1024]{1,0:T(8,128)(2,1)S(1)} %constant_dynamic-update-slice_fusion.rest_1_), channel_id=1, source_target_pairs={{0,1},{1,0},{2,3},{3,2},{4,5},{5,4},{6,7},{7,6},{8,9},{9,8},{10,11... | collective-permute-start | bytes 3145736 | tf_op jit(solution)/shard_map/ppermute | solution.py:38
  113.8 21.0 %collective-permute-start.30 = (bf16[1024,256]{1,0:T(8,128)(2,1)S(1)}, bf16[1024,256]{1,0:T(8,128)(2,1)S(1)}, u32[]{:S(2)}, u32[]{:S(2)}) collective-permute-start(bf16[1024,256]{1,0:T(8,128)(2,1)S(1)} %get-tuple-element.90), channel_id=1, source_target_pairs={{0,6},{1,7},{2,0},{3,1},{4,2},{5,3},{6,4},{7,5},{8,14},{9,15},{10,... | collective-permute-start | bytes 1572872 | tf_op jit(solution)/shard_map/ppermute | solution.py:38
  115.1 20.4 %collective-permute-start.35 = (bf16[1024,256]{1,0:T(8,128)(2,1)S(1)}, bf16[1024,256]{1,0:T(8,128)(2,1)S(1)}, u32[]{:S(2)}, u32[]{:S(2)}) collective-permute-start(bf16[1024,256]{1,0:T(8,128)(2,1)S(1)} %get-tuple-element.88), channel_id=1, source_target_pairs={{0,8},{1,9},{2,10},{3,11},{4,12},{5,13},{6,14},{7,15},{8,16},{9,17... | collective-permute-start | bytes 1572872 | tf_op jit(solution)/shard_map/ppermute | solution.py:38
  122.6 13.8 %collective-permute-start.36 = (bf16[1024,256]{1,0:T(8,128)(2,1)S(1)}, bf16[1024,256]{1,0:T(8,128)(2,1)S(1)}, u32[]{:S(2)}, u32[]{:S(2)}) collective-permute-start(bf16[1024,256]{1,0:T(8,128)(2,1)S(1)} %get-tuple-element.87), channel_id=1, source_target_pairs={{0,16},{1,17},{2,18},{3,19},{4,20},{5,21},{6,22},{7,23},{8,24},{9,... | collective-permute-start | bytes 1572872 | tf_op jit(solution)/shard_map/ppermute | solution.py:38
  134.5 15.4 %collective-permute-start.37 = (bf16[1024,256]{1,0:T(8,128)(2,1)S(1)}, bf16[1024,256]{1,0:T(8,128)(2,1)S(1)}, u32[]{:S(2)}, u32[]{:S(2)}) collective-permute-start(bf16[1024,256]{1,0:T(8,128)(2,1)S(1)} %get-tuple-element.86), channel_id=1, source_target_pairs={{0,24},{1,25},{2,26},{3,27},{4,28},{5,29},{6,30},{7,31},{8,0},{9,1... | collective-permute-start | bytes 1572872 | tf_op jit(solution)/shard_map/ppermute | solution.py:38
  134.8 41.1 %collective-permute-start.20 = (bf16[512,1024]{1,0:T(8,128)(2,1)S(1)}, bf16[512,1024]{1,0:T(8,128)(2,1)}, u32[]{:S(2)}, u32[]{:S(2)}) collective-permute-start(bf16[512,1024]{1,0:T(8,128)(2,1)S(1)} %constant_dynamic-update-slice_fusion.rest_1_), channel_id=1, source_target_pairs={{0,6},{1,25},{2,0},{3,27},{4,2},{5,29},{6,4},{7,31},{8,14},{9,1},{... | collective-permute-start | bytes 3145736 | tf_op jit(solution)/shard_map/ppermute | solution.py:55
  135.6 50.5 %collective-permute-start.22 = (bf16[512,1024]{1,0:T(8,128)(2,1)S(1)}, bf16[512,1024]{1,0:T(8,128)(2,1)}, u32[]{:S(2)}, u32[]{:S(2)}) collective-permute-start(bf16[512,1024]{1,0:T(8,128)(2,1)S(1)} %pad_maximum_fusion.rest_0_), channel_id=1, source_target_pairs={{0,2},{1,9},{2,4},{3,11},{4,6},{5,13},{6,0},{7,15},{8,10},{9,17},{... | collective-permute-start | bytes 3145736 | tf_op jit(solution)/shard_map/ppermute | solution.py:55
  136.4 50.4 %collective-permute-start.8 = (bf16[512,1024]{1,0:T(8,128)(2,1)S(1)}, bf16[512,1024]{1,0:T(8,128)(2,1)}, u32[]{:S(2)}, u32[]{:S(2)}) collective-permute-start(bf16[512,1024]{1,0:T(8,128)(2,1)S(1)} %pad_maximum_fusion.rest_0_), channel_id=1, source_target_pairs={{0,1},{1,0},{2,3},{3,2},{4,5},{5,4},{6,7},{7,6},{8,9},{9,8},{10,11... | collective-permute-start | bytes 3145736 | tf_op jit(solution)/shard_map/ppermute | solution.py:38
  149.9 37.0 %collective-permute-start.18 = (bf16[512,1024]{1,0:T(8,128)(2,1)S(1)}, bf16[512,1024]{1,0:T(8,128)(2,1)}, u32[]{:S(2)}, u32[]{:S(2)}) collective-permute-start(bf16[512,1024]{1,0:T(8,128)(2,1)S(1)} %constant_dynamic-update-slice_fusion.rest_1_), channel_id=1, source_target_pairs={{0,2},{1,9},{2,4},{3,11},{4,6},{5,13},{6,0},{7,15},{8,10},{9,17},{... | collective-permute-start | bytes 3145736 | tf_op jit(solution)/shard_map/ppermute | solution.py:55
  150.5 0.8 copy-start.6
  151.3 1.0 copy-start.1
  151.3 15.3 %collective-permute-start.38 = (bf16[1024,256]{1,0:T(8,128)(2,1)S(1)}, bf16[1024,256]{1,0:T(8,128)(2,1)S(1)}, u32[]{:S(2)}, u32[]{:S(2)}) collective-permute-start(bf16[1024,256]{1,0:T(8,128)(2,1)S(1)} %get-tuple-element.81), channel_id=1, source_target_pairs={{0,1},{1,0},{2,3},{3,2},{4,5},{5,4},{6,7},{7,6},{8,9},{9,8},{10,11... | collective-permute-start | bytes 1572872 | tf_op jit(solution)/shard_map/ppermute | solution.py:38
  166.6 0.8 copy-start.13
  167.4 24.5 %collective-permute-start.16 = (bf16[512,1024]{1,0:T(8,128)(2,1)S(1)}, bf16[512,1024]{1,0:T(8,128)(2,1)}, u32[]{:S(2)}, u32[]{:S(2)}) collective-permute-start(bf16[512,1024]{1,0:T(8,128)(2,1)S(1)} %pad_maximum_fusion.rest_0_), channel_id=1, source_target_pairs={{0,6},{1,25},{2,0},{3,27},{4,2},{5,29},{6,4},{7,31},{8,14},{9,1},{... | collective-permute-start | bytes 3145736 | tf_op jit(solution)/shard_map/ppermute | solution.py:55
  171.2 15.7 %copy-start.2 = (bf16[512,1024]{1,0:T(8,128)(2,1)S(1)}, bf16[512,1024]{1,0:T(8,128)(2,1)}, u32[]{:S(2)}) copy-start(bf16[512,1024]{1,0:T(8,128)(2,1)} %copy-done.1) | copy-start | bytes 3145732
  175.9 13.6 %collective-permute-start.39 = (f32[128,1024]{1,0:T(8,128)S(1)}, f32[128,1024]{1,0:T(8,128)S(1)}, u32[]{:S(2)}, u32[]{:S(2)}) collective-permute-start(f32[128,1024]{1,0:T(8,128)S(1)} %slice_select_fusion), channel_id=1, source_target_pairs={{0,32},{32,0},{64,96},{96,64},{1,33},{33,1},{65,97},{97,65},{2,34}... | collective-permute-start | bytes 1572872 | tf_op jit(solution)/shard_map/ppermute | solution.py:67
  186.1 26.3 %collective-permute-start.21 = (bf16[512,1024]{1,0:T(8,128)(2,1)}, bf16[512,1024]{1,0:T(8,128)(2,1)S(1)}, u32[]{:S(2)}, u32[]{:S(2)}) collective-permute-start(bf16[512,1024]{1,0:T(8,128)(2,1)} %collective-permute-done.20.rest_4_), channel_id=1, source_target_pairs={{0,1},{1,0},{2,3},{3,2},{4,5},{5,4},{6,7},{7,6},{8,9},{9,8},{10,11... | collective-permute-start | bytes 3145736 | tf_op jit(solution)/shard_map/ppermute | solution.py:38
  186.8 26.6 %collective-permute-start.14 = (bf16[512,1024]{1,0:T(8,128)(2,1)S(1)}, bf16[512,1024]{1,0:T(8,128)(2,1)}, u32[]{:S(2)}, u32[]{:S(2)}) collective-permute-start(bf16[512,1024]{1,0:T(8,128)(2,1)S(1)} %copy-done.2), channel_id=1, source_target_pairs={{0,8},{1,3},{2,10},{3,5},{4,12},{5,7},{6,14},{7,1},{8,16},{9,11},{... | collective-permute-start | bytes 3145736 | tf_op jit(solution)/shard_map/ppermute | solution.py:55
  186.9 29.2 %collective-permute-start.9 = (bf16[512,1024]{1,0:T(8,128)(2,1)}, bf16[512,1024]{1,0:T(8,128)(2,1)}, u32[]{:S(2)}, u32[]{:S(2)}) collective-permute-start(bf16[512,1024]{1,0:T(8,128)(2,1)} %collective-permute-done.8.rest_2_), channel_id=1, source_target_pairs={{0,24},{1,7},{2,26},{3,1},{4,28},{5,3},{6,30},{7,5},{8,0},{9,15},{... | collective-permute-start | bytes 3145736 | tf_op jit(solution)/shard_map/ppermute | solution.py:55
  189.5 59.3 %collective-permute-start.23 = (bf16[512,1024]{1,0:T(8,128)(2,1)}, bf16[512,1024]{1,0:T(8,128)(2,1)}, u32[]{:S(2)}, u32[]{:S(2)}) collective-permute-start(bf16[512,1024]{1,0:T(8,128)(2,1)} %collective-permute-done.22.rest_5_), channel_id=1, source_target_pairs={{0,1},{1,0},{2,3},{3,2},{4,5},{5,4},{6,7},{7,6},{8,9},{9,8},{10,11... | collective-permute-start | bytes 3145736 | tf_op jit(solution)/shard_map/ppermute | solution.py:38
  191.9 21.6 %copy-start.10 = (f32[128,1024]{1,0:T(8,128)}, f32[128,1024]{1,0:T(8,128)S(1)}, u32[]{:S(2)}) copy-start(f32[128,1024]{1,0:T(8,128)S(1)} %select_add_fusion) | copy-start | bytes 1572868
  191.9 52.3 %collective-permute-start.40 = (f32[128,1024]{1,0:T(8,128)S(1)}, f32[128,1024]{1,0:T(8,128)S(1)}, u32[]{:S(2)}, u32[]{:S(2)}) collective-permute-start(f32[128,1024]{1,0:T(8,128)S(1)} %select_add_fusion), channel_id=1, source_target_pairs={{0,64},{32,96},{64,0},{96,32},{1,65},{33,97},{65,1},{97,33},{2,66}... | collective-permute-start | bytes 1572872 | tf_op jit(solution)/shard_map/ppermute | solution.py:67
  212.4 1.0 copy-start.4
  213.4 57.8 %collective-permute-start.19 = (bf16[512,1024]{1,0:T(8,128)(2,1)}, bf16[512,1024]{1,0:T(8,128)(2,1)}, u32[]{:S(2)}, u32[]{:S(2)}) collective-permute-start(bf16[512,1024]{1,0:T(8,128)(2,1)} %collective-permute-done.18.rest_1_), channel_id=1, source_target_pairs={{0,2},{1,9},{2,4},{3,11},{4,6},{5,13},{6,0},{7,15},{8,10},{9,17},{... | collective-permute-start | bytes 3145736 | tf_op jit(solution)/shard_map/ppermute | solution.py:55
  213.4 57.8 %collective-permute-start.17 = (bf16[512,1024]{1,0:T(8,128)(2,1)}, bf16[512,1024]{1,0:T(8,128)(2,1)}, u32[]{:S(2)}, u32[]{:S(2)}) collective-permute-start(bf16[512,1024]{1,0:T(8,128)(2,1)} %collective-permute-done.16.rest_0_), channel_id=1, source_target_pairs={{0,6},{1,25},{2,0},{3,27},{4,2},{5,29},{6,4},{7,31},{8,14},{9,1},{... | collective-permute-start | bytes 3145736 | tf_op jit(solution)/shard_map/ppermute | solution.py:55
  216.1 64.0 %collective-permute-start.15 = (bf16[512,1024]{1,0:T(8,128)(2,1)}, bf16[512,1024]{1,0:T(8,128)(2,1)}, u32[]{:S(2)}, u32[]{:S(2)}) collective-permute-start(bf16[512,1024]{1,0:T(8,128)(2,1)} %collective-permute-done.14.rest_1_), channel_id=1, source_target_pairs={{0,8},{1,3},{2,10},{3,5},{4,12},{5,7},{6,14},{7,1},{8,16},{9,11},{... | collective-permute-start | bytes 3145736 | tf_op jit(solution)/shard_map/ppermute | solution.py:55
  244.1 0.8 copy-start.12
  244.9 35.2 %collective-permute-start.10 = (bf16[512,1024]{1,0:T(8,128)(2,1)}, bf16[512,1024]{1,0:T(8,128)(2,1)}, u32[]{:S(2)}, u32[]{:S(2)}) collective-permute-start(bf16[512,1024]{1,0:T(8,128)(2,1)} %collective-permute-done.9.rest_0_), channel_id=1, source_target_pairs={{0,24},{1,7},{2,26},{3,1},{4,28},{5,3},{6,30},{7,5},{8,0},{9,15},{... | collective-permute-start | bytes 3145736 | tf_op jit(solution)/shard_map/ppermute | solution.py:55
  247.5 2.5 copy-start.3
  248.9 36.4 %collective-permute-start.41 = (f32[128,1024]{1,0:T(8,128)S(1)}, f32[128,1024]{1,0:T(8,128)S(1)}, u32[]{:S(2)}, u32[]{:S(2)}) collective-permute-start(f32[128,1024]{1,0:T(8,128)S(1)} %add.896), channel_id=1, source_target_pairs={{0,32},{32,0},{64,96},{96,64},{1,33},{33,1},{65,97},{97,65},{2,34}... | collective-permute-start | bytes 1572872 | tf_op jit(solution)/shard_map/ppermute | solution.py:67
  261.1 5.2 %copy-start.5 = (bf16[512,1024]{1,0:T(8,128)(2,1)S(1)}, bf16[512,1024]{1,0:T(8,128)(2,1)}, u32[]{:S(2)}) copy-start(bf16[512,1024]{1,0:T(8,128)(2,1)} %copy-done.4) | copy-start | bytes 3145732
  285.2 1.2 copy-start.8
  285.2 1.5 copy-start.11

commit v2 on v1

--- a/solution.py
+++ b/solution.py
@@ -222,7 +222,7 @@
         ),
         input_output_aliases={2 + len(pieces): 0} if aliased else {},
         compiler_params=pltpu.CompilerParams(
-            dimension_semantics=("arbitrary",), vmem_limit_bytes=GRANT
+            dimension_semantics=("arbitrary",), vmem_limit_bytes=GRANT // 2
         ),
         cost_estimate=pl.CostEstimate(
             flops=2 * KVW * ROWS * n * SHARD, transcendentals=0, bytes_accessed=(1 << 20) + n * (3 << 18)
@@ -249,7 +249,7 @@
         out_shape=(jax.ShapeDtypeStruct((KVW, SHARD), jnp.bfloat16),) * 2,
         in_specs=[pl.BlockSpec(memory_space=pltpu.SMEM)] + [block] * 8,
         out_specs=(block, block),
-        compiler_params=pltpu.CompilerParams(vmem_limit_bytes=GRANT),
+        compiler_params=pltpu.CompilerParams(vmem_limit_bytes=GRANT // 3),
         cost_estimate=pl.CostEstimate(flops=2 << 20, transcendentals=0, bytes_accessed=5 << 20),
         name="choose",
     )(my, *parts)
@@ -279,7 +279,7 @@
         ),
         in_specs=[gt, gt, cube, cube, cube, flat],
         out_specs=(cube, flat),
-        compiler_params=pltpu.CompilerParams(vmem_limit_bytes=GRANT),
+        compiler_params=pltpu.CompilerParams(vmem_limit_bytes=GRANT // 3),
         cost_estimate=pl.CostEstimate(flops=20 << 18, transcendentals=2 << 18, bytes_accessed=7 << 20),
         name="adam",
     )(keep, recv, m, v, w, anchor)
@@ -384,8 +384,7 @@
     part = part + swap_rep(other, 1)
     part = part + swap_rep(part, 2)
     other = swap_rep(part, 1)
-    swapped = core == 1
-    total = jnp.concatenate([jnp.where(swapped, other, part), jnp.where(swapped, part, other)], axis=0)
+    total = jnp.concatenate([jnp.where(core == 0, part, other), jnp.where(core == 0, other, part)], axis=0)
     delta_avg = total / 4
     new_mom = momentum * outer_mom + delta_avg
     new_anchor = anchor - outer_rate * (delta_avg + momentum * new_mom)

time: 289 us -> 281 us (0.972)
  Pallas kernels: 62.4 us -> 56.1 us
    pallas_call x5, Pallas kernels: 35.2 us -> 28.9 us  [input_grad_part(): pl.pallas_call(functools.partial(input_grad_kernel, tuple(edges)), out_sh...]
    unnamed x32 -> x22, local copies, waits for them, and re-layouts: 7.3 us -> 5.51 us
  transfers between devices with their start and end apart: 42 -> 42, of which waited for: 13 -> 13; matrix products, arithmetic and copies ran while one was open for 2% -> 2% of each run, Pallas kernels for 19% -> 17%
where the time goes in v2:
time: 281 us; the launch traced here: 280 us
  waiting for transfers between devices  143 us (51%)
  starting transfers between devices  68.4 us (24%)
  Pallas kernels  56.1 us (20%)
  local copies, waits for them, and re-layouts  5.88 us (2%)
  other arithmetic  5.86 us (2%)
    ppermute x26, waiting for transfers between devices, send(): return lax.ppermute(value, 'fsdp', pairs)  99.5 us
    ppermute x26, starting transfers between devices, send(): return lax.ppermute(value, 'fsdp', pairs)  40.1 us
    ppermute x3, waiting for transfers between devices, swap_rep(): return lax.ppermute(value, 'rep', [(r, r ^ bit) for r in range(4)])  29 us
    pallas_call x5, Pallas kernels, input_grad_part(): pl.pallas_call(functools.partial(input_grad_kernel, tuple(edges)), out_sh...  28.9 us
    pallas_call x2, Pallas kernels, products(): pl.pallas_call(kernel, out_shape=(jax.ShapeDtypeStruct((rows, 4 * SHARD),...  20.3 us
    ppermute x13, starting transfers between devices, send_tilted(): return lax.ppermute(value, ('rep', 'fsdp'), pairs)  15.9 us
    ppermute x13, waiting for transfers between devices, send_tilted(): return lax.ppermute(value, ('rep', 'fsdp'), pairs)  14.2 us
    ppermute x3, starting transfers between devices, swap_rep(): return lax.ppermute(value, 'rep', [(r, r ^ bit) for r in range(4)])  12.4 us
  transfers between devices with their start and end apart: 42, of which 13 were waited for; matrix products, arithmetic and copies ran while one was open for 2% of the time, Pallas kernels for 17%

profile of v2, /device:TPU:1, one launch (start us, length us, event | category | flops | bytes accessed | tf_op | source)
XLA Modules:
  0.0 280.1 jit_solution(14423064796482324712)
XLA Ops:
  0.7 0.9 seq_sums.1
  1.5 3.7 %collective-permute-start = (f32[1,128]{1,0:T(1,128)S(1)}, f32[1,128]{1,0:T(1,128)S(1)}, u32[]{:S(2)}, u32[]{:S(2)}) collective-permute-start(f32[1,128]{1,0:T(1,128)S(1)} %seq_sums.1), channel_id=1, source_target_pairs={{0,1},{1,0},{2,3},{3,2},{4,5},{5,4},{6,7},{7,6},{8,9},{9,8},{10,11... | collective-permute-start | bytes 1544 | tf_op jit(solution)/shard_map/ppermute | solution.py:38
  5.3 1.0 collective-permute-done
  6.2 1.3 collective-permute-start.1
  7.5 1.4 collective-permute-start.2
  8.9 1.6 collective-permute-start.3
  10.5 1.5 copy.19
  12.2 0.6 collective-permute-done.3
  12.9 1.7 collective-permute-start.4
  14.5 2.2 collective-permute-start.5
  16.7 1.2 collective-permute-start.6
  18.2 2.5 collective-permute-done.6.v3_ref
  20.7 0.7 make_cot.1
  21.4 5.7 %shard_map.130 = (bf16[512,1024]{1,0:T(8,128)(2,1)S(1)}, bf16[512,1024]{1,0:T(8,128)(2,1)S(1)}, bf16[512,1024]{1,0:T(8,128)(2,1)S(1)}, bf16[512,1024]{1,0:T(8,128)(2,1)S(1)}) custom-call(s32[64]{0:T(128)S(1)} %stack.259.tab, bf16[1024,512]{1,0:T(8,128)(2,1)S(1)} %get-tuple-element.69.cott_ref, bf16[512,8192]{1,0:T(8,128)(2,1)} %a1.3, bf16[512,8192]{1,0:T(8,128)(2,1)} %a1.3), custom_call_target="tpu_custom_call" | custom-call | flops 2147483648 | bytes 6291456 | tf_op jit(solution)/shard_map/pallas_call | solution.py:170
  27.2 2.7 collective-permute-start.26
  29.9 2.7 collective-permute-start.33
  32.6 14.6 %shard_map.129 = (bf16[1024,1024]{1,0:T(8,128)(2,1)S(1)}, bf16[1024,1024]{1,0:T(8,128)(2,1)S(1)}, bf16[1024,1024]{1,0:T(8,128)(2,1)S(1)}, bf16[1024,1024]{1,0:T(...) custom-call(s32[64]{0:T(128)S(1)} %stack.259.tab, ...), custom_call_target="tpu_custom_call" | custom-call | flops 6442450944 | bytes 18874368 | tf_op jit(solution)/shard_map/pallas_call | solution.py:170
  47.1 1.0 collective-permute-done.24
  48.8 0.5 add_dynamic-update-slice_fusion.2
  49.3 2.7 collective-permute-start.27
  52.1 0.5 add_dynamic-update-slice_fusion.1
  52.7 0.5 add_dynamic-update-slice_fusion
  53.2 2.9 %collective-permute-start.34 = (bf16[1024,1024]{1,0:T(8,128)(2,1)S(1)}, bf16[1024,1024]{1,0:T(8,128)(2,1)S(1)}, u32[]{:S(2)}, u32[]{:S(2)}) collective-permute-start(bf16[1024,1024]{1,0:T(8,128)(2,1)S(1)} %add_dynamic-update-slice_fusion), channel_id=1, source_target_pairs={{0,6},{1,7},{2,0},{3,1},{4,2},{5,3},{6,4},{7,5},{8,14},{9,15},{10,... | collective-permute-start | bytes 6291464 | tf_op jit(solution)/shard_map/ppermute | solution.py:38
  56.3 35.9 %collective-permute-done.25 = bf16[1024,1024]{1,0:T(8,128)(2,1)S(1)} collective-permute-done((bf16[1024,1024]{1,0:T(8,128)(2,1)S(1)}, bf16[1024,1024]{1,0:T(8,128)(2,1)S(1)}, u32[]{:S(2)}, u32[]{:S(2)}) %collective-permute-start.25) | collective-permute-done | bytes 2097184 | tf_op jit(solution)/shard_map/ppermute | solution.py:38
  92.3 2.7 collective-permute-start.7
  94.9 0.8 add_convert_fusion.4
  95.7 8.2 %collective-permute-done.11 = bf16[256,1024]{1,0:T(8,128)(2,1)S(1)} collective-permute-done((bf16[256,1024]{1,0:T(8,128)(2,1)S(1)}, bf16[256,1024]{1,0:T(8,128)(2,1)S(1)}, u32[]{:S(2)}, u32[]{:S(2)}) %collective-permute-start.11) | collective-permute-done | bytes 524320 | tf_op jit(solution)/shard_map/ppermute | solution.py:55
  104.0 1.4 collective-permute-start.28
  105.4 6.0 %collective-permute-done.12 = bf16[256,1024]{1,0:T(8,128)(2,1)S(1)} collective-permute-done((bf16[256,1024]{1,0:T(8,128)(2,1)S(1)}, bf16[256,1024]{1,0:T(8,128)(2,1)S(1)}, u32[]{:S(2)}, u32[]{:S(2)}) %collective-permute-start.12) | collective-permute-done | bytes 524320 | tf_op jit(solution)/shard_map/ppermute | solution.py:55
  111.4 0.6 collective-permute-start.29
  112.0 1.7 collective-permute-start.13
  113.8 0.6 collective-permute-start.30
  114.4 0.8 add_convert_fusion
  115.3 7.3 %collective-permute-done.28.refs_1_ = bf16[1024,256]{1,0:T(8,128)(2,1)S(1)} collective-permute-done((bf16[1024,256]{1,0:T(8,128)(2,1)S(1)}, bf16[1024,256]{1,0:T(8,128)(2,1)S(1)}, u32[]{:S(2)}, u32[]{:S(2)}) %collective-permute-start.28) | collective-permute-done | bytes 524320 | tf_op jit(solution)/shard_map/ppermute | solution.py:38
  122.6 2.2 collective-permute-start.36
  124.8 9.6 %collective-permute-done.29.refs_2_ = bf16[1024,256]{1,0:T(8,128)(2,1)S(1)} collective-permute-done((bf16[1024,256]{1,0:T(8,128)(2,1)S(1)}, bf16[1024,256]{1,0:T(8,128)(2,1)S(1)}, u32[]{:S(2)}, u32[]{:S(2)}) %collective-permute-start.29) | collective-permute-done | bytes 524320 | tf_op jit(solution)/shard_map/ppermute | solution.py:38
  134.7 0.8 collective-permute-start.20
  135.6 0.7 collective-permute-start.22
  136.3 5.9 %collective-permute-start.8 = (bf16[512,1024]{1,0:T(8,128)(2,1)S(1)}, bf16[512,1024]{1,0:T(8,128)(2,1)}, u32[]{:S(2)}, u32[]{:S(2)}) collective-permute-start(bf16[512,1024]{1,0:T(8,128)(2,1)S(1)} %pad_maximum_fusion.rest_0_), channel_id=1, source_target_pairs={{0,1},{1,0},{2,3},{3,2},{4,5},{5,4},{6,7},{7,6},{8,9},{9,8},{10,11... | collective-permute-start | bytes 3145736 | tf_op jit(solution)/shard_map/ppermute | solution.py:38
  142.2 7.5 %collective-permute-done.37.refs_7_ = bf16[1024,256]{1,0:T(8,128)(2,1)S(1)} collective-permute-done((bf16[1024,256]{1,0:T(8,128)(2,1)S(1)}, bf16[1024,256]{1,0:T(8,128)(2,1)S(1)}, u32[]{:S(2)}, u32[]{:S(2)}) %collective-permute-start.37) | collective-permute-done | bytes 524320 | tf_op jit(solution)/shard_map/ppermute | solution.py:38
  149.7 0.6 choose.1
  150.3 0.8 copy-done.3
  151.1 1.0 copy-done.1
  152.1 14.4 %collective-permute-done.38.recv_ref = bf16[1024,256]{1,0:T(8,128)(2,1)S(1)} collective-permute-done((bf16[1024,256]{1,0:T(8,128)(2,1)S(1)}, bf16[1024,256]{1,0:T(8,128)(2,1)S(1)}, u32[]{:S(2)}, u32[]{:S(2)}) %collective-permute-start.38) | collective-permute-done | bytes 524320 | tf_op jit(solution)/shard_map/ppermute | solution.py:38
  166.5 0.8 copy-done.8
  167.3 3.7 %collective-permute-start.16 = (bf16[512,1024]{1,0:T(8,128)(2,1)S(1)}, bf16[512,1024]{1,0:T(8,128)(2,1)}, u32[]{:S(2)}, u32[]{:S(2)}) collective-permute-start(bf16[512,1024]{1,0:T(8,128)(2,1)S(1)} %pad_maximum_fusion.rest_0_), channel_id=1, source_target_pairs={{0,6},{1,25},{2,0},{3,27},{4,2},{5,29},{6,4},{7,31},{8,14},{9,1},{... | collective-permute-start | bytes 3145736 | tf_op jit(solution)/shard_map/ppermute | solution.py:55
  171.0 4.7 %adam.1 = (f32[1,256,1024]{2,1,0:T(8,128)}, f32[256,1024]{1,0:T(8,128)S(1)}) custom-call(bf16[1024,256]{1,0:T(8,128)(2,1)} %copy-done.3, bf16[1024,256]{1,0:T(8,128)(2,1)} %copy-done.8, f32[1,256,1024]{2,1,0:T(8,128)} %m_ref.1, f32[1,256,1024]{2,1,0:T(8,128)} %v_ref.1, f32[1,256,1024]{2,1,0:T(8,128)} %w_ref.1, f32[256,1024]{1,0:T(8,128)} %anchor_ref.1), custom_call_target="tpu_custom_call" | custom-call | flops 5242880 | bytes 7340032 | tf_op jit(solution)/shard_map/adam/pallas_call | solution.py:273
  175.7 10.3 %collective-permute-start.39 = (f32[128,1024]{1,0:T(8,128)S(1)}, f32[128,1024]{1,0:T(8,128)S(1)}, u32[]{:S(2)}, u32[]{:S(2)}) collective-permute-start(f32[128,1024]{1,0:T(8,128)S(1)} %slice_select_fusion), channel_id=1, source_target_pairs={{0,32},{32,0},{64,96},{96,64},{1,33},{33,1},{65,97},{97,65},{2,34}... | collective-permute-start | bytes 1572872 | tf_op jit(solution)/shard_map/ppermute | solution.py:67
  186.0 0.8 collective-permute-start.21
  186.9 2.7 collective-permute-start.9
  189.6 2.1 collective-permute-start.23
  191.8 0.9 collective-permute-start.40
  192.7 19.6 %collective-permute-done.21.rest_0_ = bf16[512,1024]{1,0:T(8,128)(2,1)S(1)} collective-permute-done((bf16[512,1024]{1,0:T(8,128)(2,1)}, bf16[512,1024]{1,0:T(8,128)(2,1)S(1)}, u32[]{:S(2)}, u32[]{:S(2)}) %collective-permute-start.21) | collective-permute-done | bytes 1048608 | tf_op jit(solution)/shard_map/ppermute | solution.py:38
  212.4 2.7 collective-permute-start.17
  215.0 29.0 %collective-permute-done.40 = f32[128,1024]{1,0:T(8,128)S(1)} collective-permute-done((f32[128,1024]{1,0:T(8,128)S(1)}, f32[128,1024]{1,0:T(8,128)S(1)}, u32[]{:S(2)}, u32[]{:S(2)}) %collective-permute-start.40) | collective-permute-done | bytes 524320 | tf_op jit(solution)/shard_map/ppermute | solution.py:67
  244.1 2.6 collective-permute-start.10
  246.7 1.2 collective-permute-start.41
  247.9 11.0 %input_grad.5.rest_2_ = bf16[512,8192]{1,0:T(8,128)(2,1)} custom-call(s32[64]{0:T(128)S(1)} %stack.259.tab, bf16[512,1024]{1,0:T(8,128)(2,1)S(1)} %get-tuple-element.68.cot_ref, bf16[512,1024]{1,0:T(8,128)(2,1)S(1)} %pad_maximum_fusion.rest_0_, bf16[512,1024]{1,0:T(8,128)(2,1)S(1)} %constant_dynamic-update-slice_fusion.rest_1_, ...), custom_call_target="tpu_custom_call" | custom-call | flops 3221225472 | bytes 10485760 | tf_op jit(solution)/shard_map/input_grad/pallas_call | solution.py:209
  259.0 5.2 %input_grad.6.rest_2_ = bf16[512,8192]{1,0:T(8,128)(2,1)} custom-call(s32[64]{0:T(128)S(1)} %stack.259.tab, bf16[512,1024]{1,0:T(8,128)(2,1)S(1)} %get-tuple-element.68.cot_ref, bf16[512,1024]{1,0:T(8,128)(2,1)} %collective-permute-done.16.rest_0_, bf16[512,1024]{1,0:T(8,128)(2,1)} %collective-permute-done.18.rest_1_, ...), custom_call_target="tpu_custom_call", output_to_operand_aliasing={{}: (4, {})} | custom-call | flops 1073741824 | bytes 4194304 | tf_op jit(solution)/shard_map/input_grad/pallas_call | solution.py:209
  264.1 3.4 %input_grad.7.rest_4_ = bf16[512,8192]{1,0:T(8,128)(2,1)} custom-call(s32[64]{0:T(128)S(1)} %stack.259.tab, bf16[512,1024]{1,0:T(8,128)(2,1)S(1)} %get-tuple-element.68.cot_ref, bf16[512,1024]{1,0:T(8,128)(2,1)S(1)} %collective-permute-done.21.rest_0_, bf16[512,1024]{1,0:T(8,128)(2,1)S(1)} %collective-permute-done.23.rest_1_, ...), custom_call_target="tpu_custom_call", output_to_operand_aliasing={{}: (4, {})} | custom-call | flops 1073741824 | bytes 4194304 | tf_op jit(solution)/shard_map/input_grad/pallas_call | solution.py:209
  267.6 5.8 %input_grad.8.rest_2_ = bf16[512,8192]{1,0:T(8,128)(2,1)} custom-call(s32[64]{0:T(128)S(1)} %stack.259.tab, bf16[512,1024]{1,0:T(8,128)(2,1)S(1)} %get-tuple-element.68.cot_ref, bf16[512,1024]{1,0:T(8,128)(2,1)S(1)} %collective-permute-done.9.rest_0_, bf16[512,1024]{1,0:T(8,128)(2,1)S(1)} %collective-permute-done.14.rest_1_, ...), custom_call_target="tpu_custom_call", output_to_operand_aliasing={{}: (6, {})} | custom-call | flops 2147483648 | bytes 7340032 | tf_op jit(solution)/shard_map/input_grad/pallas_call | solution.py:209
  273.4 3.4 %input_grad.9 = bf16[512,8192]{1,0:T(8,128)(2,1)} custom-call(s32[64]{0:T(128)S(1)} %stack.259.tab, bf16[512,1024]{1,0:T(8,128)(2,1)S(1)} %get-tuple-element.68.cot_ref, bf16[512,1024]{1,0:T(8,128)(2,1)S(1)} %collective-permute-done.10.rest_0_, bf16[512,1024]{1,0:T(8,128)(2,1)S(1)} %collective-permute-done.15.rest_1_, ...), custom_call_target="tpu_custom_call", output_to_operand_aliasing={{}: (4, {})} | custom-call | flops 1073741824 | bytes 4194304 | tf_op jit(solution)/shard_map/input_grad/pallas_call | solution.py:209
  277.0 1.1 copy-done.5
  278.4 1.7 multiply_subtract_fusion
  (72 shorter events, 2.6 us)
Async XLA Ops:
  0.6 11.4 %copy-start.4 = (s32[512]{0:T(512)S(1)}, s32[512]{0:T(512)}, u32[]{:S(2)}) copy-start(s32[512]{0:T(512)} %param.21) | copy-start | bytes 6148
  0.6 20.0 %copy-start = (bf16[512,1024]{1,0:T(8,128)(2,1)S(1)}, bf16[512,1024]{1,0:T(8,128)(2,1)}, u32[]{:S(2)}) copy-start(bf16[512,1024]{1,0:T(8,128)(2,1)} %tg_ref.1) | copy-start | bytes 3145732
  0.7 11.5 %copy-start.9 = (s32[1,32]{1,0:T(1,128)S(1)}, s32[1,32]{1,0:T(1,128)}, u32[]{:S(2)}) copy-start(s32[1,32]{1,0:T(1,128)} %param.22) | copy-start | bytes 388
  1.5 4.7 %collective-permute-start = (f32[1,128]{1,0:T(1,128)S(1)}, f32[1,128]{1,0:T(1,128)S(1)}, u32[]{:S(2)}, u32[]{:S(2)}) collective-permute-start(f32[1,128]{1,0:T(1,128)S(1)} %seq_sums.1), channel_id=1, source_target_pairs={{0,1},{1,0},{2,3},{3,2},{4,5},{5,4},{6,7},{7,6},{8,9},{9,8},{10,11... | collective-permute-start | bytes 1544 | tf_op jit(solution)/shard_map/ppermute | solution.py:38
  6.2 5.9 %collective-permute-start.1 = (f32[1,128]{1,0:T(1,128)S(1)}, f32[1,128]{1,0:T(1,128)S(1)}, u32[]{:S(2)}, u32[]{:S(2)}) collective-permute-start(f32[1,128]{1,0:T(1,128)S(1)} %add.871), channel_id=1, source_target_pairs={{0,8},{1,9},{2,10},{3,11},{4,12},{5,13},{6,14},{7,15},{8,16},{9,17... | collective-permute-start | bytes 1544 | tf_op jit(solution)/shard_map/ppermute | solution.py:38
  7.5 4.7 %collective-permute-start.2 = (f32[1,128]{1,0:T(1,128)S(1)}, f32[1,128]{1,0:T(1,128)S(1)}, u32[]{:S(2)}, u32[]{:S(2)}) collective-permute-start(f32[1,128]{1,0:T(1,128)S(1)} %add.871), channel_id=1, source_target_pairs={{0,24},{1,25},{2,26},{3,27},{4,28},{5,29},{6,30},{7,31},{8,0},{9,1... | collective-permute-start | bytes 1544 | tf_op jit(solution)/shard_map/ppermute | solution.py:38
  8.9 3.9 %collective-permute-start.3 = (f32[1,128]{1,0:T(1,128)S(1)}, f32[1,128]{1,0:T(1,128)S(1)}, u32[]{:S(2)}, u32[]{:S(2)}) collective-permute-start(f32[1,128]{1,0:T(1,128)S(1)} %add.871), channel_id=1, source_target_pairs={{0,16},{1,17},{2,18},{3,19},{4,20},{5,21},{6,22},{7,23},{8,24},{9,... | collective-permute-start | bytes 1544 | tf_op jit(solution)/shard_map/ppermute | solution.py:38
  12.9 5.3 %collective-permute-start.4 = (f32[1,128]{1,0:T(1,128)S(1)}, f32[1,128]{1,0:T(1,128)S(1)}, u32[]{:S(2)}, u32[]{:S(2)}) collective-permute-start(f32[1,128]{1,0:T(1,128)S(1)} %add_add_fusion.v0_ref), channel_id=1, source_target_pairs={{0,2},{1,3},{2,4},{3,5},{4,6},{5,7},{6,0},{7,1},{8,10},{9,11},{10,... | collective-permute-start | bytes 1544 | tf_op jit(solution)/shard_map/ppermute | solution.py:38
  14.5 3.6 %collective-permute-start.5 = (f32[1,128]{1,0:T(1,128)S(1)}, f32[1,128]{1,0:T(1,128)S(1)}, u32[]{:S(2)}, u32[]{:S(2)}) collective-permute-start(f32[1,128]{1,0:T(1,128)S(1)} %add_add_fusion.v0_ref), channel_id=1, source_target_pairs={{0,6},{1,7},{2,0},{3,1},{4,2},{5,3},{6,4},{7,5},{8,14},{9,15},{10,... | collective-permute-start | bytes 1544 | tf_op jit(solution)/shard_map/ppermute | solution.py:38
  16.7 3.9 %collective-permute-start.6 = (f32[1,128]{1,0:T(1,128)S(1)}, f32[1,128]{1,0:T(1,128)S(1)}, u32[]{:S(2)}, u32[]{:S(2)}) collective-permute-start(f32[1,128]{1,0:T(1,128)S(1)} %add_add_fusion.v0_ref), channel_id=1, source_target_pairs={{0,4},{1,5},{2,6},{3,7},{4,0},{5,1},{6,2},{7,3},{8,12},{9,13},{10,... | collective-permute-start | bytes 1544 | tf_op jit(solution)/shard_map/ppermute | solution.py:38
  27.1 21.0 %collective-permute-start.24 = (bf16[512,1024]{1,0:T(8,128)(2,1)S(1)}, bf16[512,1024]{1,0:T(8,128)(2,1)S(1)}, u32[]{:S(2)}, u32[]{:S(2)}) collective-permute-start(bf16[512,1024]{1,0:T(8,128)(2,1)S(1)} %get-tuple-element.72), channel_id=1, source_target_pairs={{0,8},{1,9},{2,10},{3,11},{4,12},{5,13},{6,14},{7,15},{8,16},{9,17... | collective-permute-start | bytes 3145736 | tf_op jit(solution)/shard_map/ppermute | solution.py:38
  27.2 21.6 %collective-permute-start.26 = (bf16[512,1024]{1,0:T(8,128)(2,1)S(1)}, bf16[512,1024]{1,0:T(8,128)(2,1)S(1)}, u32[]{:S(2)}, u32[]{:S(2)}) collective-permute-start(bf16[512,1024]{1,0:T(8,128)(2,1)S(1)} %get-tuple-element.74), channel_id=1, source_target_pairs={{0,24},{1,25},{2,26},{3,27},{4,28},{5,29},{6,30},{7,31},{8,0},{9,1... | collective-permute-start | bytes 3145736 | tf_op jit(solution)/shard_map/ppermute | solution.py:38
  29.9 22.2 %collective-permute-start.31 = (bf16[512,1024]{1,0:T(8,128)(2,1)S(1)}, bf16[512,1024]{1,0:T(8,128)(2,1)S(1)}, u32[]{:S(2)}, u32[]{:S(2)}) collective-permute-start(bf16[512,1024]{1,0:T(8,128)(2,1)S(1)} %get-tuple-element.77), channel_id=1, source_target_pairs={{0,2},{1,3},{2,4},{3,5},{4,6},{5,7},{6,0},{7,1},{8,10},{9,11},{10,... | collective-permute-start | bytes 3145736 | tf_op jit(solution)/shard_map/ppermute | solution.py:38
  29.9 22.8 %collective-permute-start.33 = (bf16[512,1024]{1,0:T(8,128)(2,1)S(1)}, bf16[512,1024]{1,0:T(8,128)(2,1)S(1)}, u32[]{:S(2)}, u32[]{:S(2)}) collective-permute-start(bf16[512,1024]{1,0:T(8,128)(2,1)S(1)} %get-tuple-element.79), channel_id=1, source_target_pairs={{0,6},{1,7},{2,0},{3,1},{4,2},{5,3},{6,4},{7,5},{8,14},{9,15},{10,... | collective-permute-start | bytes 3145736 | tf_op jit(solution)/shard_map/ppermute | solution.py:38
  48.7 43.6 %collective-permute-start.25 = (bf16[1024,1024]{1,0:T(8,128)(2,1)S(1)}, bf16[1024,1024]{1,0:T(8,128)(2,1)S(1)}, u32[]{:S(2)}, u32[]{:S(2)}) collective-permute-start(bf16[1024,1024]{1,0:T(8,128)(2,1)S(1)} %add_dynamic-update-slice_fusion.3), channel_id=1, source_target_pairs={{0,8},{1,9},{2,10},{3,11},{4,12},{5,13},{6,14},{7,15},{8,16},{9,17... | collective-permute-start | bytes 6291464 | tf_op jit(solution)/shard_map/ppermute | solution.py:38
  49.3 42.9 %collective-permute-start.27 = (bf16[1024,1024]{1,0:T(8,128)(2,1)S(1)}, bf16[1024,1024]{1,0:T(8,128)(2,1)S(1)}, u32[]{:S(2)}, u32[]{:S(2)}) collective-permute-start(bf16[1024,1024]{1,0:T(8,128)(2,1)S(1)} %add_dynamic-update-slice_fusion.2), channel_id=1, source_target_pairs={{0,24},{1,25},{2,26},{3,27},{4,28},{5,29},{6,30},{7,31},{8,0},{9,1... | collective-permute-start | bytes 6291464 | tf_op jit(solution)/shard_map/ppermute | solution.py:38
  52.6 3.5 %copy-start.6 = (f32[1,256,1024]{2,1,0:T(8,128)S(1)}, f32[1,256,1024]{2,1,0:T(8,128)}, u32[]{:S(2)}) copy-start(f32[1,256,1024]{2,1,0:T(8,128)} %w_ref.1) | copy-start | bytes 3145732
  52.6 59.4 %collective-permute-start.32 = (bf16[1024,1024]{1,0:T(8,128)(2,1)S(1)}, bf16[1024,1024]{1,0:T(8,128)(2,1)S(1)}, u32[]{:S(2)}, u32[]{:S(2)}) collective-permute-start(bf16[1024,1024]{1,0:T(8,128)(2,1)S(1)} %add_dynamic-update-slice_fusion.1), channel_id=1, source_target_pairs={{0,2},{1,3},{2,4},{3,5},{4,6},{5,7},{6,0},{7,1},{8,10},{9,11},{10,... | collective-permute-start | bytes 6291464 | tf_op jit(solution)/shard_map/ppermute | solution.py:38
  53.2 60.5 %collective-permute-start.34 = (bf16[1024,1024]{1,0:T(8,128)(2,1)S(1)}, bf16[1024,1024]{1,0:T(8,128)(2,1)S(1)}, u32[]{:S(2)}, u32[]{:S(2)}) collective-permute-start(bf16[1024,1024]{1,0:T(8,128)(2,1)S(1)} %add_dynamic-update-slice_fusion), channel_id=1, source_target_pairs={{0,6},{1,7},{2,0},{3,1},{4,2},{5,3},{6,4},{7,5},{8,14},{9,15},{10,... | collective-permute-start | bytes 6291464 | tf_op jit(solution)/shard_map/ppermute | solution.py:38
  56.2 47.8 %collective-permute-start.11 = (bf16[256,1024]{1,0:T(8,128)(2,1)S(1)}, bf16[256,1024]{1,0:T(8,128)(2,1)S(1)}, u32[]{:S(2)}, u32[]{:S(2)}) collective-permute-start(bf16[256,1024]{1,0:T(8,128)(2,1)S(1)} %convert_bitcast_fusion), channel_id=1, source_target_pairs={{0,16},{1,5},{2,18},{3,7},{4,20},{5,1},{6,22},{7,3},{8,24},{9,13},... | collective-permute-start | bytes 1572872 | tf_op jit(solution)/shard_map/ppermute | solution.py:55
  92.2 19.1 %collective-permute-start.12 = (bf16[256,1024]{1,0:T(8,128)(2,1)S(1)}, bf16[256,1024]{1,0:T(8,128)(2,1)S(1)}, u32[]{:S(2)}, u32[]{:S(2)}) collective-permute-start(bf16[256,1024]{1,0:T(8,128)(2,1)S(1)} %convert_bitcast_fusion), channel_id=1, source_target_pairs={{0,8},{1,3},{2,10},{3,5},{4,12},{5,7},{6,14},{7,1},{8,16},{9,11},{... | collective-permute-start | bytes 1572872 | tf_op jit(solution)/shard_map/ppermute | solution.py:55
  92.3 22.9 %collective-permute-start.7 = (bf16[256,1024]{1,0:T(8,128)(2,1)S(1)}, bf16[256,1024]{1,0:T(8,128)(2,1)S(1)}, u32[]{:S(2)}, u32[]{:S(2)}) collective-permute-start(bf16[256,1024]{1,0:T(8,128)(2,1)S(1)} %convert_bitcast_fusion), channel_id=1, source_target_pairs={{0,24},{1,7},{2,26},{3,1},{4,28},{5,3},{6,30},{7,5},{8,0},{9,15},{... | collective-permute-start | bytes 1572872 | tf_op jit(solution)/shard_map/ppermute | solution.py:55
  104.0 18.6 %collective-permute-start.28 = (bf16[1024,256]{1,0:T(8,128)(2,1)S(1)}, bf16[1024,256]{1,0:T(8,128)(2,1)S(1)}, u32[]{:S(2)}, u32[]{:S(2)}) collective-permute-start(bf16[1024,256]{1,0:T(8,128)(2,1)S(1)} %get-tuple-element.92), channel_id=1, source_target_pairs={{0,2},{1,3},{2,4},{3,5},{4,6},{5,7},{6,0},{7,1},{8,10},{9,11},{10,... | collective-permute-start | bytes 1572872 | tf_op jit(solution)/shard_map/ppermute | solution.py:38
  111.4 23.0 %collective-permute-start.29 = (bf16[1024,256]{1,0:T(8,128)(2,1)S(1)}, bf16[1024,256]{1,0:T(8,128)(2,1)S(1)}, u32[]{:S(2)}, u32[]{:S(2)}) collective-permute-start(bf16[1024,256]{1,0:T(8,128)(2,1)S(1)} %get-tuple-element.91), channel_id=1, source_target_pairs={{0,4},{1,5},{2,6},{3,7},{4,0},{5,1},{6,2},{7,3},{8,12},{9,13},{10,... | collective-permute-start | bytes 1572872 | tf_op jit(solution)/shard_map/ppermute | solution.py:38
  112.0 39.1 %collective-permute-start.13 = (bf16[512,1024]{1,0:T(8,128)(2,1)S(1)}, bf16[512,1024]{1,0:T(8,128)(2,1)S(1)}, u32[]{:S(2)}, u32[]{:S(2)}) collective-permute-start(bf16[512,1024]{1,0:T(8,128)(2,1)S(1)} %constant_dynamic-update-slice_fusion.rest_1_), channel_id=1, source_target_pairs={{0,1},{1,0},{2,3},{3,2},{4,5},{5,4},{6,7},{7,6},{8,9},{9,8},{10,11... | collective-permute-start | bytes 3145736 | tf_op jit(solution)/shard_map/ppermute | solution.py:38
  113.8 20.9 %collective-permute-start.30 = (bf16[1024,256]{1,0:T(8,128)(2,1)S(1)}, bf16[1024,256]{1,0:T(8,128)(2,1)S(1)}, u32[]{:S(2)}, u32[]{:S(2)}) collective-permute-start(bf16[1024,256]{1,0:T(8,128)(2,1)S(1)} %get-tuple-element.90), channel_id=1, source_target_pairs={{0,6},{1,7},{2,0},{3,1},{4,2},{5,3},{6,4},{7,5},{8,14},{9,15},{10,... | collective-permute-start | bytes 1572872 | tf_op jit(solution)/shard_map/ppermute | solution.py:38
  115.2 20.4 %collective-permute-start.35 = (bf16[1024,256]{1,0:T(8,128)(2,1)S(1)}, bf16[1024,256]{1,0:T(8,128)(2,1)S(1)}, u32[]{:S(2)}, u32[]{:S(2)}) collective-permute-start(bf16[1024,256]{1,0:T(8,128)(2,1)S(1)} %get-tuple-element.88), channel_id=1, source_target_pairs={{0,8},{1,9},{2,10},{3,11},{4,12},{5,13},{6,14},{7,15},{8,16},{9,17... | collective-permute-start | bytes 1572872 | tf_op jit(solution)/shard_map/ppermute | solution.py:38
  122.6 13.7 %collective-permute-start.36 = (bf16[1024,256]{1,0:T(8,128)(2,1)S(1)}, bf16[1024,256]{1,0:T(8,128)(2,1)S(1)}, u32[]{:S(2)}, u32[]{:S(2)}) collective-permute-start(bf16[1024,256]{1,0:T(8,128)(2,1)S(1)} %get-tuple-element.87), channel_id=1, source_target_pairs={{0,16},{1,17},{2,18},{3,19},{4,20},{5,21},{6,22},{7,23},{8,24},{9,... | collective-permute-start | bytes 1572872 | tf_op jit(solution)/shard_map/ppermute | solution.py:38
  134.3 15.3 %collective-permute-start.37 = (bf16[1024,256]{1,0:T(8,128)(2,1)S(1)}, bf16[1024,256]{1,0:T(8,128)(2,1)S(1)}, u32[]{:S(2)}, u32[]{:S(2)}) collective-permute-start(bf16[1024,256]{1,0:T(8,128)(2,1)S(1)} %get-tuple-element.86), channel_id=1, source_target_pairs={{0,24},{1,25},{2,26},{3,27},{4,28},{5,29},{6,30},{7,31},{8,0},{9,1... | collective-permute-start | bytes 1572872 | tf_op jit(solution)/shard_map/ppermute | solution.py:38
  134.7 41.1 %collective-permute-start.20 = (bf16[512,1024]{1,0:T(8,128)(2,1)S(1)}, bf16[512,1024]{1,0:T(8,128)(2,1)}, u32[]{:S(2)}, u32[]{:S(2)}) collective-permute-start(bf16[512,1024]{1,0:T(8,128)(2,1)S(1)} %constant_dynamic-update-slice_fusion.rest_1_), channel_id=1, source_target_pairs={{0,6},{1,25},{2,0},{3,27},{4,2},{5,29},{6,4},{7,31},{8,14},{9,1},{... | collective-permute-start | bytes 3145736 | tf_op jit(solution)/shard_map/ppermute | solution.py:55
  135.6 50.5 %collective-permute-start.22 = (bf16[512,1024]{1,0:T(8,128)(2,1)S(1)}, bf16[512,1024]{1,0:T(8,128)(2,1)}, u32[]{:S(2)}, u32[]{:S(2)}) collective-permute-start(bf16[512,1024]{1,0:T(8,128)(2,1)S(1)} %pad_maximum_fusion.rest_0_), channel_id=1, source_target_pairs={{0,2},{1,9},{2,4},{3,11},{4,6},{5,13},{6,0},{7,15},{8,10},{9,17},{... | collective-permute-start | bytes 3145736 | tf_op jit(solution)/shard_map/ppermute | solution.py:55
  136.3 50.6 %collective-permute-start.8 = (bf16[512,1024]{1,0:T(8,128)(2,1)S(1)}, bf16[512,1024]{1,0:T(8,128)(2,1)}, u32[]{:S(2)}, u32[]{:S(2)}) collective-permute-start(bf16[512,1024]{1,0:T(8,128)(2,1)S(1)} %pad_maximum_fusion.rest_0_), channel_id=1, source_target_pairs={{0,1},{1,0},{2,3},{3,2},{4,5},{5,4},{6,7},{7,6},{8,9},{9,8},{10,11... | collective-permute-start | bytes 3145736 | tf_op jit(solution)/shard_map/ppermute | solution.py:38
  149.7 37.2 %collective-permute-start.18 = (bf16[512,1024]{1,0:T(8,128)(2,1)S(1)}, bf16[512,1024]{1,0:T(8,128)(2,1)}, u32[]{:S(2)}, u32[]{:S(2)}) collective-permute-start(bf16[512,1024]{1,0:T(8,128)(2,1)S(1)} %constant_dynamic-update-slice_fusion.rest_1_), channel_id=1, source_target_pairs={{0,2},{1,9},{2,4},{3,11},{4,6},{5,13},{6,0},{7,15},{8,10},{9,17},{... | collective-permute-start | bytes 3145736 | tf_op jit(solution)/shard_map/ppermute | solution.py:55
  150.3 0.8 copy-start.3
  151.1 1.0 copy-start.1
  151.1 15.4 %collective-permute-start.38 = (bf16[1024,256]{1,0:T(8,128)(2,1)S(1)}, bf16[1024,256]{1,0:T(8,128)(2,1)S(1)}, u32[]{:S(2)}, u32[]{:S(2)}) collective-permute-start(bf16[1024,256]{1,0:T(8,128)(2,1)S(1)} %get-tuple-element.81), channel_id=1, source_target_pairs={{0,1},{1,0},{2,3},{3,2},{4,5},{5,4},{6,7},{7,6},{8,9},{9,8},{10,11... | collective-permute-start | bytes 1572872 | tf_op jit(solution)/shard_map/ppermute | solution.py:38
  166.5 0.8 copy-start.8
  167.3 24.5 %collective-permute-start.16 = (bf16[512,1024]{1,0:T(8,128)(2,1)S(1)}, bf16[512,1024]{1,0:T(8,128)(2,1)}, u32[]{:S(2)}, u32[]{:S(2)}) collective-permute-start(bf16[512,1024]{1,0:T(8,128)(2,1)S(1)} %pad_maximum_fusion.rest_0_), channel_id=1, source_target_pairs={{0,6},{1,25},{2,0},{3,27},{4,2},{5,29},{6,4},{7,31},{8,14},{9,1},{... | collective-permute-start | bytes 3145736 | tf_op jit(solution)/shard_map/ppermute | solution.py:55
  171.0 15.9 %copy-start.2 = (bf16[512,1024]{1,0:T(8,128)(2,1)S(1)}, bf16[512,1024]{1,0:T(8,128)(2,1)}, u32[]{:S(2)}) copy-start(bf16[512,1024]{1,0:T(8,128)(2,1)} %copy-done.1) | copy-start | bytes 3145732
  175.7 13.8 %collective-permute-start.39 = (f32[128,1024]{1,0:T(8,128)S(1)}, f32[128,1024]{1,0:T(8,128)S(1)}, u32[]{:S(2)}, u32[]{:S(2)}) collective-permute-start(f32[128,1024]{1,0:T(8,128)S(1)} %slice_select_fusion), channel_id=1, source_target_pairs={{0,32},{32,0},{64,96},{96,64},{1,33},{33,1},{65,97},{97,65},{2,34}... | collective-permute-start | bytes 1572872 | tf_op jit(solution)/shard_map/ppermute | solution.py:67
  186.0 26.3 %collective-permute-start.21 = (bf16[512,1024]{1,0:T(8,128)(2,1)}, bf16[512,1024]{1,0:T(8,128)(2,1)S(1)}, u32[]{:S(2)}, u32[]{:S(2)}) collective-permute-start(bf16[512,1024]{1,0:T(8,128)(2,1)} %collective-permute-done.20.rest_4_), channel_id=1, source_target_pairs={{0,1},{1,0},{2,3},{3,2},{4,5},{5,4},{6,7},{7,6},{8,9},{9,8},{10,11... | collective-permute-start | bytes 3145736 | tf_op jit(solution)/shard_map/ppermute | solution.py:38
  186.9 25.5 %collective-permute-start.14 = (bf16[512,1024]{1,0:T(8,128)(2,1)S(1)}, bf16[512,1024]{1,0:T(8,128)(2,1)S(1)}, u32[]{:S(2)}, u32[]{:S(2)}) collective-permute-start(bf16[512,1024]{1,0:T(8,128)(2,1)S(1)} %copy-done.2), channel_id=1, source_target_pairs={{0,8},{1,3},{2,10},{3,5},{4,12},{5,7},{6,14},{7,1},{8,16},{9,11},{... | collective-permute-start | bytes 3145736 | tf_op jit(solution)/shard_map/ppermute | solution.py:55
  186.9 28.1 %collective-permute-start.9 = (bf16[512,1024]{1,0:T(8,128)(2,1)}, bf16[512,1024]{1,0:T(8,128)(2,1)S(1)}, u32[]{:S(2)}, u32[]{:S(2)}) collective-permute-start(bf16[512,1024]{1,0:T(8,128)(2,1)} %collective-permute-done.8.rest_2_), channel_id=1, source_target_pairs={{0,24},{1,7},{2,26},{3,1},{4,28},{5,3},{6,30},{7,5},{8,0},{9,15},{... | collective-permute-start | bytes 3145736 | tf_op jit(solution)/shard_map/ppermute | solution.py:55
  189.6 57.1 %collective-permute-start.23 = (bf16[512,1024]{1,0:T(8,128)(2,1)}, bf16[512,1024]{1,0:T(8,128)(2,1)S(1)}, u32[]{:S(2)}, u32[]{:S(2)}) collective-permute-start(bf16[512,1024]{1,0:T(8,128)(2,1)} %collective-permute-done.22.rest_5_), channel_id=1, source_target_pairs={{0,1},{1,0},{2,3},{3,2},{4,5},{5,4},{6,7},{7,6},{8,9},{9,8},{10,11... | collective-permute-start | bytes 3145736 | tf_op jit(solution)/shard_map/ppermute | solution.py:38
  191.8 52.3 %collective-permute-start.40 = (f32[128,1024]{1,0:T(8,128)S(1)}, f32[128,1024]{1,0:T(8,128)S(1)}, u32[]{:S(2)}, u32[]{:S(2)}) collective-permute-start(f32[128,1024]{1,0:T(8,128)S(1)} %select_add_fusion), channel_id=1, source_target_pairs={{0,64},{32,96},{64,0},{96,32},{1,65},{33,97},{65,1},{97,33},{2,66}... | collective-permute-start | bytes 1572872 | tf_op jit(solution)/shard_map/ppermute | solution.py:67
  212.4 55.2 %collective-permute-start.19 = (bf16[512,1024]{1,0:T(8,128)(2,1)}, bf16[512,1024]{1,0:T(8,128)(2,1)S(1)}, u32[]{:S(2)}, u32[]{:S(2)}) collective-permute-start(bf16[512,1024]{1,0:T(8,128)(2,1)} %collective-permute-done.18.rest_1_), channel_id=1, source_target_pairs={{0,2},{1,9},{2,4},{3,11},{4,6},{5,13},{6,0},{7,15},{8,10},{9,17},{... | collective-permute-start | bytes 3145736 | tf_op jit(solution)/shard_map/ppermute | solution.py:55
  212.4 55.2 %collective-permute-start.17 = (bf16[512,1024]{1,0:T(8,128)(2,1)}, bf16[512,1024]{1,0:T(8,128)(2,1)S(1)}, u32[]{:S(2)}, u32[]{:S(2)}) collective-permute-start(bf16[512,1024]{1,0:T(8,128)(2,1)} %collective-permute-done.16.rest_0_), channel_id=1, source_target_pairs={{0,6},{1,25},{2,0},{3,27},{4,2},{5,29},{6,4},{7,31},{8,14},{9,1},{... | collective-permute-start | bytes 3145736 | tf_op jit(solution)/shard_map/ppermute | solution.py:55
  215.0 58.4 %collective-permute-start.15 = (bf16[512,1024]{1,0:T(8,128)(2,1)S(1)}, bf16[512,1024]{1,0:T(8,128)(2,1)S(1)}, u32[]{:S(2)}, u32[]{:S(2)}) collective-permute-start(bf16[512,1024]{1,0:T(8,128)(2,1)S(1)} %collective-permute-done.14.rest_1_), channel_id=1, source_target_pairs={{0,8},{1,3},{2,10},{3,5},{4,12},{5,7},{6,14},{7,1},{8,16},{9,11},{... | collective-permute-start | bytes 3145736 | tf_op jit(solution)/shard_map/ppermute | solution.py:55
  244.1 29.3 %collective-permute-start.10 = (bf16[512,1024]{1,0:T(8,128)(2,1)S(1)}, bf16[512,1024]{1,0:T(8,128)(2,1)S(1)}, u32[]{:S(2)}, u32[]{:S(2)}) collective-permute-start(bf16[512,1024]{1,0:T(8,128)(2,1)S(1)} %collective-permute-done.9.rest_0_), channel_id=1, source_target_pairs={{0,24},{1,7},{2,26},{3,1},{4,28},{5,3},{6,30},{7,5},{8,0},{9,15},{... | collective-permute-start | bytes 3145736 | tf_op jit(solution)/shard_map/ppermute | solution.py:55
  246.7 30.1 %collective-permute-start.41 = (f32[128,1024]{1,0:T(8,128)S(1)}, f32[128,1024]{1,0:T(8,128)S(1)}, u32[]{:S(2)}, u32[]{:S(2)}) collective-permute-start(f32[128,1024]{1,0:T(8,128)S(1)} %add.896), channel_id=1, source_target_pairs={{0,32},{32,0},{64,96},{96,64},{1,33},{33,1},{65,97},{97,65},{2,34}... | collective-permute-start | bytes 1572872 | tf_op jit(solution)/shard_map/ppermute | solution.py:67
  276.9 1.2 copy-start.5
  276.9 1.5 copy-start.7
